TPU v7x, 32 devices: a whole 2x2x4 slice. The times are simulated.
32 devices in a mesh: row: 4 (over x, core), col: 8 (over z, y).
Axes of the slice: x: 2, y: 2, z: 4, core: 2. Of those that a mesh axis runs over, the one named last changes fastest.
Arguments:
- object_slices: float32 [2, 2, 1024, 2048], P(None, None, 'row', 'col'), may hold values from -5 to 5
- probe: float32 [2, 128, 128], replicated, may hold values from -6 to 6
- amplitudes: float32 [4, 8, 16, 128, 128], P('row', 'col'), may hold values from 0.3 to 3
- scan_pos: int32 [2, 4, 8, 16], P(None, 'row', 'col'), may hold values from 0 to 2047, as said below
- scan_count: int32 [4, 8], P('row', 'col'), may hold values from 0 to 16, as said below
Outputs:
- object_new: float32 [2, 2, 1024, 2048], P(None, None, 'row', 'col')
Inputs may be any that keep to these rules, and one draw needn't show every extreme that they name: `scan_pos`: entry [0, i, j, k] is the pixel row and [1, i, j, k] the pixel column of the centre of slot k of tile (i, j); the centre lies within that tile's 256 x 256 pixels, also for slots that are not live. The live scans of a tile are its first scan_count slots; in every tile row the counts of its 8 tiles sum to exactly 64, and some tile of every row holds 16 scans.
All inputs are finite; a program needn't handle non-finite values.
Results may differ from a plain program's by a relative error of at most 0.00029.
Values sent between devices are 32-bit elements; how exact they have to be, the bound alone decides.
No kernel may reach another device: no remote copies, remote signals or barrier semaphores. Data moves between devices by JAX's collectives and lax.ppermute only.
A program may use at most 128 MiB of HBM per device.

v0:
```python
import math

import jax
import jax.numpy as jnp
import ml_dtypes
import numpy as np
from jax import lax
from jax.experimental import pallas as pl
from jax.experimental.pallas import tpu as pltpu
from jax.sharding import PartitionSpec as P

ITERS = 2
LANES = 128
GROUP = 8

modulus_offset = 0.5
fresnel_scale = 0.9


def split_table(table):
    high = table.astype(np.float32).astype(ml_dtypes.bfloat16)
    low = (table - high.astype(np.float64)).astype(np.float32).astype(ml_dtypes.bfloat16)
    return high, low


def transform_tables(frame_size):
    positions = np.arange(frame_size)
    dft = np.exp(-2j * math.pi * (positions[:, None] * positions[None, :] % frame_size) / frame_size)
    dft = dft / math.sqrt(frame_size)
    frequency = np.where(positions < frame_size // 2, positions, positions - frame_size)
    phase = np.exp(1j * math.pi * fresnel_scale * frequency.astype(np.float64) ** 2 / frame_size)
    hop = (np.conj(dft) * phase[None, :]) @ dft
    half = frame_size // 2
    hop_parts = ((hop[:half, :half] + hop[:half, half:]) / 2, (hop[:half, :half] - hop[:half, half:]) / 2)
    into = (dft[0::2, :half], dft[1::2, :half])
    out_of = (np.conj(dft[:half, 0::2]), np.conj(dft[:half, 1::2]))
    rights, lefts = [], []
    for matrix in (dft, np.conj(dft), hop, np.conj(hop)):
        rights.extend(
            split_table(np.block([[matrix.real, matrix.imag], [-matrix.imag, matrix.real]]))
        )
    for parts in (into, out_of, hop_parts, np.conj(hop_parts)):
        for part in parts:
            lefts.append(
                np.concatenate(
                    split_table(np.block([[part.real, -part.imag], [part.imag, part.real]]))
                )
            )
    return np.stack(rights), np.stack(lefts)


DFT, INVERSE, HOP, HOP_BACK = 0, 1, 2, 3


def exchange(odd_values, even_values, axis):
    count = lax.axis_size(axis)
    received = []
    for values, first in ((odd_values, 1), (even_values, 0)):
        lower = range(first, count - 1, 2)
        pairs = [(i, i + 1) for i in lower] + [(i + 1, i) for i in lower]
        received.append(lax.ppermute(values, axis, pairs))
    return received


def paired(axis, before, after):
    even = lax.rem(lax.axis_index(axis), 2) == 0
    return jnp.where(even, before, after), jnp.where(even, after, before)


def lane_ids(shape):
    return lax.broadcasted_iota(jnp.int32, shape, len(shape) - 1)


def swap_halves(values):
    return pltpu.roll(values, LANES // 2, values.ndim - 1)


def vmem():
    return pl.BlockSpec(memory_space=pltpu.VMEM)


def smem():
    return pl.BlockSpec(memory_space=pltpu.SMEM)


def split(values):
    high = values.astype(jnp.bfloat16)
    return high, (values - high.astype(jnp.float32)).astype(jnp.bfloat16)


def dot(a, b):
    return jnp.dot(a, b, preferred_element_type=jnp.float32)


def blend(first, second):
    return jnp.where(lane_ids(first.shape) < LANES // 2, first, second)


def segments(rows, rim):
    half = rows // 2
    return ((slice(0, rim), slice(rows - rim, rows)), (slice(rim, half), slice(half, rows - rim)))


def pack_kernel(*refs):
    count = (len(refs) - 8) // 3
    sources, outs, targets = refs[: count + 1], refs[count + 1 : count + 8], refs[count + 8 : -count - 2]
    turned_ref, odd_edge, even_edge, odd_mid, even_mid, row_odd, row_even = outs
    object_ref, sems = refs[-count - 2], refs[-count - 1 :]
    copies = [
        pltpu.make_async_copy(source, target, sem)
        for source, target, sem in zip(sources, (object_ref, *targets), sems)
    ]
    for copy in copies:
        copy.start()
    copies[0].wait()
    planes, rows, cols = object_ref.shape
    tiles = cols // LANES
    pieces = segments(rows, odd_edge.shape[1])
    for plane in range(planes):
        for (upper, lower), odd_ref, even_ref in zip(
            pieces, (odd_edge, odd_mid), (even_edge, even_mid)
        ):
            left = blend(
                object_ref[plane, lower, 0:LANES], swap_halves(object_ref[plane, upper, 0:LANES])
            )
            right = blend(
                swap_halves(object_ref[plane, upper, cols - LANES : cols]),
                object_ref[plane, lower, cols - LANES : cols],
            )
            odd_ref[plane], even_ref[plane] = paired("col", left, right)
    for plane in range(planes):
        for tile in range(tiles):
            turned = swap_halves(object_ref[plane, :, tile * LANES : (tile + 1) * LANES])
            turned_ref[plane, tile] = turned
            upper, lower = pieces[0]
            row_odd[plane, tile], row_even[plane, tile] = paired("row", turned[upper], turned[lower])
    for copy in copies[1:]:
        copy.wait()


def lay(turned_ref, plane, rows, left, right, field_ref, row_at):
    tiles = turned_ref.shape[1]
    parts = [left] + [turned_ref[plane, tile, rows, :] for tile in range(tiles)] + [right]
    for block in range(tiles + 1):
        field_ref[plane, block, row_at : row_at + rows.stop - rows.start, :] = blend(
            parts[block], parts[block + 1]
        )


def corner_kernel(from_odd, from_even, odd_ref, even_ref):
    for plane in range(odd_ref.shape[0]):
        left, right = paired("col", from_odd[plane], from_even[plane])
        odd_ref[plane], even_ref[plane] = paired(
            "row", blend(left, right), swap_halves(blend(right, left))
        )


def gradients(pos_ref, count_ref, amps_ref, probe_ref, rights_ref, lefts_ref, field_ref, grad_ref, work):
    frame = probe_ref.shape[-1]
    o0, o1, inc, wave = work
    count = count_ref[0, 0]
    first_row = lax.axis_index("row") * (field_ref.shape[2] - frame)
    first_col = lax.axis_index("col") * ((field_ref.shape[1] - 1) * LANES)
    lanes = lane_ids((frame, LANES))

    grad_ref[...] = jnp.zeros_like(grad_ref)

    half = frame // 2

    def right(source, kind):
        table_high, table_low = rights_ref[2 * kind], rights_ref[2 * kind + 1]
        high, low = split(source)
        return dot(high, table_high) + (dot(low, table_high) + dot(high, table_low))

    def left(re, im, kind):
        upper, lower = (re[:half], im[:half]), (re[half:], im[half:])
        if kind != INVERSE:
            upper, lower = (
                [a + b for a, b in zip(upper, lower)], [a - b for a, b in zip(upper, lower)]
            )
        sides = []
        for side, (side_re, side_im) in enumerate((upper, lower)):
            table = lefts_ref[2 * kind + side]
            high, low = split(jnp.concatenate([side_re, side_im], axis=0))
            out = dot(
                jnp.concatenate([table, table], axis=1), jnp.concatenate([high, low], axis=0)
            )
            out = out[:frame] + out[frame:]
            sides.append((out[:half], out[half:]))
        upper, lower = sides
        if kind != DFT:
            upper, lower = (
                [a + b for a, b in zip(upper, lower)], [a - b for a, b in zip(upper, lower)]
            )
        return [jnp.concatenate([a, b], axis=0) for a, b in zip(upper, lower)]

    def two_sided(zs, kind):
        outs = [
            right(
                jnp.concatenate([jnp.concatenate(z, axis=1) for z in zs[pair : pair + 2]], axis=0),
                kind,
            )
            for pair in range(0, len(zs), 2)
        ]
        mixes = [
            left(
                jnp.concatenate([out[:frame, :frame], out[frame:, :frame]], axis=1),
                jnp.concatenate([out[:frame, frame:], out[frame:, frame:]], axis=1),
                kind,
            )
            for out in outs
        ]
        return [
            (re[:, k * frame : (k + 1) * frame], im[:, k * frame : (k + 1) * frame])
            for re, im in mixes
            for k in range(2)
        ]

    def group_step(group, carry):
        base = group * GROUP
        where = []
        for k in range(GROUP):
            row_at = pos_ref[0, 0, 0, base + k] - first_row
            col_at = pos_ref[1, 0, 0, base + k] - first_col
            block = lax.shift_right_logical(col_at, 7)
            shift = jnp.bitwise_and(col_at, LANES - 1)
            where.append((pl.ds(row_at, frame), block, shift))
            for plane in range(4):
                near = field_ref[plane, block, pl.ds(row_at, frame), :]
                far = field_ref[plane, block + 1, pl.ds(row_at, frame), :]
                joined = jnp.where(lanes >= shift, near, far)
                target = o0 if plane < 2 else o1
                target[k, plane % 2] = pltpu.roll(
                    joined, jnp.bitwise_and(LANES - shift, LANES - 1), 1
                )
        probe_re, probe_im = probe_ref[0], probe_ref[1]
        zs = []
        for k in range(GROUP):
            a, b = o0[k, 0], o0[k, 1]
            zs.append((probe_re * a - probe_im * b, probe_re * b + probe_im * a))
        for k, (re, im) in enumerate(two_sided(zs, HOP)):
            inc[k, 0] = re
            inc[k, 1] = im
        zs = []
        for k in range(GROUP):
            a, b, c, d = inc[k, 0], inc[k, 1], o1[k, 0], o1[k, 1]
            zs.append((a * c - b * d, a * d + b * c))
        for k, (re, im) in enumerate(two_sided(zs, DFT)):
            live = jnp.where(base + k < count, 1.0, 0.0)
            amps = jnp.concatenate(
                [amps_ref[base + k, pl.ds(odd, half, stride=2), :] for odd in range(2)], axis=0
            )
            factor = (1.0 - amps * lax.rsqrt(re * re + im * im + modulus_offset)) * live
            wave[k, 0] = re * factor
            wave[k, 1] = im * factor
        zs = [(wave[k, 0], wave[k, 1]) for k in range(GROUP)]

        def place(k, first_plane, values):
            rows, block, shift = where[k]
            for part in range(2):
                moved = pltpu.roll(values[part], shift, 1)
                near = jnp.where(lanes >= shift, moved, 0.0)
                far = jnp.where(lanes >= shift, 0.0, moved)
                grad_ref[first_plane + part, block, rows, :] += near
                grad_ref[first_plane + part, block + 1, rows, :] += far

        for k, (re, im) in enumerate(two_sided(zs, INVERSE)):
            wave[k, 0] = re
            wave[k, 1] = im
        zs = []
        for k in range(GROUP):
            re, im = wave[k, 0], wave[k, 1]
            a, b, c, d = inc[k, 0], inc[k, 1], o1[k, 0], o1[k, 1]
            place(k, 2, (a * re + b * im, a * im - b * re))
            zs.append((c * re + d * im, c * im - d * re))
        for k, (re, im) in enumerate(two_sided(zs, HOP_BACK)):
            place(k, 0, (probe_re * re + probe_im * im, probe_re * im - probe_im * re))
        return carry

    lax.fori_loop(0, (count + GROUP - 1) // GROUP, group_step, 0)


def outer(blocks):
    return (0, blocks - 1)


def inner(blocks):
    return range(1, blocks - 1)


def write_grad(grad_ref, pieces):
    left, mid, right, band_odd, band_even = pieces[-5:]
    _, blocks, all_rows, _ = grad_ref.shape
    rim = pieces[0].shape[-2]
    rows = all_rows - 2 * rim
    if len(pieces) == 8:
        row_odd, row_even, edges = pieces[:3]
        groups = [(row_odd, row_even, edges, [(0, blocks - 1), (blocks - 1, 0), *inner(blocks)])]
    else:
        row_odd, row_even, row_mid_odd, row_mid_even, edges, edges_mid = pieces[:6]
        groups = [
            (row_odd, row_even, edges, outer(blocks)),
            (row_mid_odd, row_mid_even, edges_mid, inner(blocks)),
        ]

    def rows_of(block, lo):
        if isinstance(block, tuple):
            return blend(*[grad_ref[:, part, lo : lo + rim, :] for part in block])
        return grad_ref[:, block, lo : lo + rim, :]

    for odd, even, edge, group in groups:
        for at, block in enumerate(group):
            odd[:, at], even[:, at] = paired("row", rows_of(block, 0), rows_of(block, rows + rim))
            edge[:, at, 0:rim, :] = rows_of(block, rim)
            edge[:, at, rim : 2 * rim, :] = rows_of(block, rows)
    left[...] = grad_ref[:, 0, 2 * rim : rows, :]
    mid[...] = grad_ref[:, 1 : blocks - 1, 2 * rim : rows, :]
    right[...] = grad_ref[:, blocks - 1, 2 * rim : rows, :]
    if band_odd.shape[1] == rows - 2 * rim:
        band_odd[...], band_even[...] = paired("col", left[...], right[...])
    else:
        half = (rows - 2 * rim) // 2
        upper, lower = slice(2 * rim, 2 * rim + half), slice(2 * rim + half, rows)
        pack_bands(grad_ref, (band_odd, band_even), upper, lower)


def pack_bands(ref, packed, upper, lower):
    last = ref.shape[1] - 1
    for plane in range(ref.shape[0]):
        packed[0][plane], packed[1][plane] = paired(
            "col",
            blend(ref[plane, 0, upper, :], swap_halves(ref[plane, 0, lower, :])),
            blend(swap_halves(ref[plane, last, lower, :]), ref[plane, last, upper, :]),
        )


def first_kernel(
    pos_ref, count_ref, turned_ref, edge_odd, edge_even, mid_odd, mid_even, row_odd, row_even,
    corner_odd, corner_even, amps_ref, probe_ref, rights_ref, lefts_ref, field_ref, *rest,
):
    pieces, (grad_ref, *work) = rest[:-5], rest[-5:]
    planes, _, rows, _ = turned_ref.shape
    rim = edge_odd.shape[1]
    for plane in range(planes):
        for (upper, lower), odd, even in zip(
            segments(rows, rim), (edge_odd, mid_odd), (edge_even, mid_even)
        ):
            left, right = paired("col", odd[plane], even[plane])
            lay(turned_ref, plane, upper, left, right, field_ref, rim + upper.start)
            left, right = swap_halves(left), swap_halves(right)
            lay(turned_ref, plane, lower, left, right, field_ref, rim + lower.start)
        corners = paired("row", corner_odd[plane], corner_even[plane])
        rims = paired("row", row_odd[plane], row_even[plane])
        for strip, corner, row_at in zip(rims, corners, (0, rows + rim)):
            parts = [corner, *strip, corner]
            for block in range(len(parts) - 1):
                field_ref[plane, block, row_at : row_at + rim, :] = blend(
                    parts[block], parts[block + 1]
                )
    gradients(pos_ref, count_ref, amps_ref, probe_ref, rights_ref, lefts_ref, field_ref, grad_ref, work)
    write_grad(grad_ref, pieces)


def fold(edges, row_odd, row_even, plane, at):
    rim = row_odd.shape[2]
    from_up, from_down = paired("row", row_odd[plane, at], row_even[plane, at])
    return edges[plane, at, 0:rim, :] + from_up, edges[plane, at, rim : 2 * rim, :] + from_down


def fold_kernel(edges, row_odd, row_even, folded_ref, odd_ref, even_ref):
    planes, count = edges.shape[:2]
    rim = row_odd.shape[2]
    for plane in range(planes):
        for at in range(count):
            upper, lower = fold(edges, row_odd, row_even, plane, at)
            folded_ref[plane, at, 0:rim, :] = upper
            folded_ref[plane, at, rim : 2 * rim, :] = lower
    odd_ref[...], even_ref[...] = paired("col", folded_ref[:, 0], folded_ref[:, count - 1])


def last_fold_kernel(edges, row_odd, row_even, odd_ref, even_ref):
    for plane in range(edges.shape[0]):
        upper, lower = fold(edges, row_odd, row_even, plane, 0)
        lower = swap_halves(lower)
        odd_ref[plane], even_ref[plane] = paired("col", blend(upper, lower), blend(lower, upper))


def fold_mid_kernel(edges, row_odd, row_even, up_ref, down_ref, odd_ref, even_ref):
    for plane in range(edges.shape[0]):
        for at in range(edges.shape[1]):
            upper, lower = fold(edges, row_odd, row_even, plane, at)
            up_ref[plane, at], down_ref[plane, at] = upper, lower
            odd_ref[plane, at], even_ref[plane, at] = paired("row", upper, lower)


def total_kernel(folded_ref, from_odd, from_even, up_ref, down_ref, odd_ref, even_ref):
    planes, count, rim, _ = up_ref.shape
    for plane in range(planes):
        sides = paired("col", from_odd[plane], from_even[plane])
        for at in range(count):
            values = folded_ref[plane, at] + sides[at]
            upper, lower = values[0:rim], values[rim : 2 * rim]
            up_ref[plane, at], down_ref[plane, at] = upper, lower
            odd_ref[plane, at], even_ref[plane, at] = paired("row", upper, lower)


def next_kernel(
    pos_ref, count_ref, old_ref, up_ref, down_ref, up_mid, down_mid, left_ref, mid_ref, right_ref,
    from_odd, from_even, row_odd, row_even, row_mid_odd, row_mid_even,
    amps_ref, probe_ref, rights_ref, lefts_ref, field_ref, *rest,
):
    pieces, (grad_ref, *work) = rest[:-5], rest[-5:]
    _, blocks, all_rows, _ = old_ref.shape
    rim = up_ref.shape[2]
    rows = all_rows - 2 * rim
    from_left, from_right = paired("col", from_odd[...], from_even[...])
    for block in range(blocks):
        lane = lane_ids((1, 1, LANES))
        inside = lane >= 0
        if block in inner(blocks):
            at, odd, even, up, down = block - 1, row_mid_odd, row_mid_even, up_mid, down_mid
            middle = mid_ref[:, at]
        elif block == 0:
            at, odd, even, up, down = 0, row_odd, row_even, up_ref, down_ref
            inside = lane >= jnp.where(lax.axis_index("col") == 0, LANES // 2, 0)
            middle = left_ref[...] + from_left
        else:
            at, odd, even, up, down = 1, row_odd, row_even, up_ref, down_ref
            at_end = lax.axis_index("col") == lax.axis_size("col") - 1
            inside = lane < jnp.where(at_end, LANES // 2, LANES)
            middle = right_ref[...] + from_right
        from_up, from_down = paired("row", odd[:, at], even[:, at])
        for lo, hi, values in (
            (0, rim, from_up),
            (rim, 2 * rim, up[:, at]),
            (2 * rim, rows, middle),
            (rows, rows + rim, down[:, at]),
            (rows + rim, all_rows, from_down),
        ):
            updated = old_ref[:, block, lo:hi, :] - values
            field_ref[:, block, lo:hi, :] = jnp.where(inside, updated, 0.0)
    gradients(pos_ref, count_ref, amps_ref, probe_ref, rights_ref, lefts_ref, field_ref, grad_ref, work)
    write_grad(grad_ref, pieces)


def put_rows(field_ref, plane, row_at, values, sides, part, target_ref, put_at):
    size = values[0].shape[0]
    if part == 1:
        sides = [swap_halves(side) for side in sides]
    values = [values[0] + sides[0], *values[1:-1], values[-1] + sides[1]]
    turned = [
        swap_halves(field_ref[plane, block, row_at : row_at + size, :] - block_values)
        for block, block_values in enumerate(values)
    ]
    for block in range(len(turned) - 1):
        target_ref[plane, put_at : put_at + size, block * LANES : (block + 1) * LANES] = blend(
            turned[block], turned[block + 1]
        )


def finish_mid_kernel(
    field_ref, left_ref, mid_ref, right_ref, from_odd, from_even, out_hbm, result, sem
):
    planes, blocks, all_rows, _ = field_ref.shape
    band = result.shape[1]
    rim = (all_rows - band) // 4
    half = band // 2
    for plane in range(planes):
        sides = paired("col", from_odd[plane], from_even[plane])
        for part in range(2):
            at = slice(part * half, (part + 1) * half)
            values = [left_ref[plane, at, :], right_ref[plane, at, :]]
            values[1:1] = [mid_ref[plane, k, at, :] for k in range(blocks - 2)]
            put_rows(
                field_ref, plane, 2 * rim + part * half, values, sides, part, result, part * half
            )
    copy = pltpu.make_async_copy(result, out_hbm.at[:, rim : rim + band, :], sem)
    copy.start()
    copy.wait()


def finish_edge_kernel(
    field_ref, edges, row_odd, row_even, from_odd, from_even, _, out_hbm, result, *sems
):
    planes, blocks, all_rows, _ = field_ref.shape
    rim = from_odd.shape[1]
    rows = all_rows - 2 * rim
    copies = []
    for part in range(2):
        for plane in range(planes):
            sides = paired("col", from_odd[plane], from_even[plane])
            folded = [fold(edges, row_odd, row_even, plane, k)[part] for k in range(1, blocks)]
            values = [*folded, folded[0]]
            put_rows(
                field_ref, plane, rim + part * (rows - rim), values, sides, part, result, part * rim
            )
        at = part * (rows - rim)
        copies.append(
            pltpu.make_async_copy(
                result.at[:, part * rim : (part + 1) * rim, :],
                out_hbm.at[:, at : at + rim, :],
                sems[part],
            )
        )
        copies[-1].start()
    for copy in copies:
        copy.wait()


def f32(*shape):
    return pltpu.VMEM(shape, jnp.float32)


def on_chip(*arrays):
    return [pltpu.with_memory_space_constraint(array, pltpu.VMEM) for array in arrays]


def body(object_slices, probe, amplitudes, scan_pos, scan_count):
    layers, _, tile_r, tile_c = object_slices.shape
    planes = layers * 2
    frame = probe.shape[-1]
    rim = frame // 2
    blocks = tile_c // LANES + 1
    slots = amplitudes.shape[2]
    assert slots % GROUP == 0
    amps = amplitudes[0, 0]
    scalars = [scan_pos, scan_count]
    tables = [jnp.asarray(table) for table in transform_tables(frame)]
    tile = object_slices.reshape(planes, tile_r, tile_c)

    band = tile_r - 2 * rim

    def call(kernel, outs, mib, scratch=(), scalars=(), raw=(), in_hbm=False, alias=None):
        def run(*arrays):
            return pl.pallas_call(
                kernel,
                out_shape=outs,
                input_output_aliases=alias or {},
                in_specs=[smem()] * len(scalars) + [vmem()] * len(arrays)
                + [pl.BlockSpec(memory_space=pltpu.HBM)] * len(raw),
                out_specs=[pl.BlockSpec(memory_space=pltpu.HBM) if in_hbm else vmem()] * len(outs),
                scratch_shapes=list(scratch),
                compiler_params=pltpu.CompilerParams(vmem_limit_bytes=mib << 20),
            )(
                *scalars,
                *on_chip(*arrays),
                *[pltpu.with_memory_space_constraint(array, pltpu.HBM) for array in raw],
            )

        return run

    packed_edge = f32(planes, rim, LANES)
    packed_mid = f32(planes, band // 2, LANES)
    row_strip = f32(planes, blocks - 1, rim, LANES)
    constants = (amps, probe, *tables)
    turned, odd_edge, even_edge, odd_mid, even_mid, odd, even, amps, probe, *tables = call(
        pack_kernel,
        [f32(planes, blocks - 1, tile_r, LANES)]
        + [packed_edge] * 2 + [packed_mid] * 2 + [row_strip] * 2
        + [pltpu.VMEM(array.shape, array.dtype) for array in constants],
        8,
        scratch=[f32(planes, tile_r, tile_c)]
        + [pltpu.SemaphoreType.DMA(())] * (len(constants) + 1),
        raw=[tile, *constants],
    )()
    edge_strips = exchange(odd_edge, even_edge, "col")
    row_strips = exchange(odd, even, "row")
    mid_strips = exchange(odd_mid, even_mid, "col")
    odd, even = call(corner_kernel, [packed_edge] * 2, 4)(*edge_strips)
    corner_strips = exchange(odd, even, "row")

    field_shape = f32(planes, blocks, tile_r + frame, LANES)
    work = [field_shape] + [pltpu.VMEM((GROUP, 2, frame, frame), jnp.float32)] * 4
    strip, strip_mid = f32(planes, 2, rim, LANES), f32(planes, blocks - 2, rim, LANES)
    edge_rows = f32(planes, 2, 2 * rim, LANES)
    band_rows = f32(planes, band, LANES)
    pieces = [strip] * 2 + [strip_mid] * 2 + [
        edge_rows,
        f32(planes, blocks - 2, 2 * rim, LANES),
        band_rows,
        f32(planes, blocks - 2, band, LANES),
        band_rows,
    ]
    field, *grads = call(
        first_kernel,
        [field_shape] + pieces + [band_rows] * 2,
        20,
        scratch=work,
        scalars=scalars,
    )(turned, *edge_strips, *mid_strips, *row_strips, *corner_strips, amps, probe, *tables)

    for iteration in range(1, ITERS):
        odd, even, odd_in, even_in, edges, edges_mid, left, mid, right, band_odd, band_even = grads
        row_strips = exchange(odd, even, "row")
        mid_strips = exchange(band_odd, band_even, "col")
        inner_strips = exchange(odd_in, even_in, "row")
        edges, odd, even = call(
            fold_kernel, [edge_rows] + [f32(planes, 2 * rim, LANES)] * 2, 4
        )(edges, *row_strips)
        edge_strips = exchange(odd, even, "col")
        up_mid, down_mid, odd_in, even_in = call(fold_mid_kernel, [strip_mid] * 4, 4)(
            edges_mid, *inner_strips
        )
        inner_strips = exchange(odd_in, even_in, "row")
        up, down, odd, even = call(total_kernel, [strip] * 4, 4)(edges, *edge_strips)
        row_strips = exchange(odd, even, "row")
        if iteration < ITERS - 1:
            outs = pieces + [band_rows] * 2
        else:
            outs = [f32(planes, blocks, rim, LANES)] * 2 + [
                f32(planes, blocks, 2 * rim, LANES),
                *pieces[6:],
                packed_mid,
                packed_mid,
            ]
        field, *grads = call(
            next_kernel, [field_shape] + outs, 20, scratch=work, scalars=scalars
        )(
            field, up, down, up_mid, down_mid, left, mid, right,
            *mid_strips, *row_strips, *inner_strips, amps, probe, *tables,
        )

    odd, even, edges, left, mid, right, band_odd, band_even = grads
    row_strips = exchange(odd, even, "row")
    mid_strips = exchange(band_odd, band_even, "col")
    odd, even = call(last_fold_kernel, [packed_edge] * 2, 4)(edges, *row_strips)
    edge_strips = exchange(odd, even, "col")
    whole = pltpu.HBM((planes, tile_r, tile_c), jnp.float32)
    (out,) = call(
        finish_mid_kernel,
        [whole],
        4,
        scratch=[f32(planes, band, tile_c), pltpu.SemaphoreType.DMA(())],
        in_hbm=True,
    )(field, left, mid, right, *mid_strips)
    (out,) = call(
        finish_edge_kernel,
        [whole],
        4,
        scratch=[f32(planes, 2 * rim, tile_c)] + [pltpu.SemaphoreType.DMA(())] * 2,
        raw=[out],
        in_hbm=True,
        alias={6: 0},
    )(field, edges, *row_strips, *edge_strips)
    return out.reshape(object_slices.shape)


def solution(mesh):
    in_specs = (
        P(None, None, "row", "col"),
        P(),
        P("row", "col", None, None, None),
        P(None, "row", "col", None),
        P("row", "col"),
    )
    out_specs = P(None, None, "row", "col")

    return jax.shard_map(body, mesh=mesh, in_specs=in_specs, out_specs=out_specs, check_vma=False)
```

profile of v0, /device:TPU:25, one launch (start us, length us, event | category | flops | bytes accessed | tf_op | source)
XLA Modules:
  0.0 98.0 jit_solution(16569430488584676702)
XLA Ops:
  0.0 2.1 %shard_map.73 = (f32[4,2,256,128]{3,2,1,0:T(8,128)S(1)}, f32[4,64,128]{2,1,0:T(8,128)S(1)}, f32[4,64,128]{2,1,0:T(8,128)S(1)}, f32[4,64,128]{2,1,0:T(8,128)S(1)}...) custom-call(f32[4,256,256]{2,1,0:T(8,128)} %bitcast.3, ...), custom_call_target="tpu_custom_call" | custom-call | tf_op jit(solution)/shard_map/pallas_call | solution.py:535
  2.1 3.0 %collective-permute-start = (f32[4,64,128]{2,1,0:T(8,128)S(1)}, f32[4,64,128]{2,1,0:T(8,128)S(1)}, u32[]{:S(2)}, u32[]{:S(2)}) collective-permute-start(f32[4,64,128]{2,1,0:T(8,128)S(1)} %get-tuple-element.53), channel_id=1, source_target_pairs={{1,2},{3,4},{5,6},{2,1},{4,3},{6,5},{9,10},{11,12},{13,14},{10,9},... | collective-permute-start | bytes 393224 | tf_op jit(solution)/shard_map/ppermute | solution.py:61
  5.2 3.2 %collective-permute-start.2 = (f32[4,64,128]{2,1,0:T(8,128)S(1)}, f32[4,64,128]{2,1,0:T(8,128)S(1)}, u32[]{:S(2)}, u32[]{:S(2)}) collective-permute-start(f32[4,64,128]{2,1,0:T(8,128)S(1)} %get-tuple-element.55), channel_id=1, source_target_pairs={{1,2},{3,4},{5,6},{2,1},{4,3},{6,5},{9,10},{11,12},{13,14},{10,9},... | collective-permute-start | bytes 393224 | tf_op jit(solution)/shard_map/ppermute | solution.py:61
  8.5 4.5 %collective-permute-start.4 = (f32[4,2,64,128]{3,2,1,0:T(8,128)S(1)}, f32[4,2,64,128]{3,2,1,0:T(8,128)S(1)}, u32[]{:S(2)}, u32[]{:S(2)}) collective-permute-start(f32[4,2,64,128]{3,2,1,0:T(8,128)S(1)} %get-tuple-element.57), channel_id=1, source_target_pairs={{8,16},{16,8},{9,17},{17,9},{10,18},{18,10},{11,19},{19,11},{12,20... | collective-permute-start | bytes 786440 | tf_op jit(solution)/shard_map/ppermute | solution.py:61
  13.2 2.8 %collective-permute-done.1.from_even.edge_even = f32[4,64,128]{2,1,0:T(8,128)S(1)} collective-permute-done((f32[4,64,128]{2,1,0:T(8,128)S(1)}, f32[4,64,128]{2,1,0:T(8,128)S(1)}, u32[]{:S(2)}, u32[]{:S(2)}) %collective-permute-start.1) | collective-permute-done | bytes 131104 | tf_op jit(solution)/shard_map/ppermute | solution.py:61
  16.0 3.6 %collective-permute-start.6 = (f32[4,64,128]{2,1,0:T(8,128)S(1)}, f32[4,64,128]{2,1,0:T(8,128)S(1)}, u32[]{:S(2)}, u32[]{:S(2)}) collective-permute-start(f32[4,64,128]{2,1,0:T(8,128)S(1)} %get-tuple-element.59), channel_id=1, source_target_pairs={{8,16},{16,8},{9,17},{17,9},{10,18},{18,10},{11,19},{19,11},{12,20... | collective-permute-start | bytes 393224 | tf_op jit(solution)/shard_map/ppermute | solution.py:61
  20.4 1.9 %collective-permute-done.6.corner_odd = f32[4,64,128]{2,1,0:T(8,128)S(1)} collective-permute-done((f32[4,64,128]{2,1,0:T(8,128)S(1)}, f32[4,64,128]{2,1,0:T(8,128)S(1)}, u32[]{:S(2)}, u32[]{:S(2)}) %collective-permute-start.6) | collective-permute-done | bytes 131104 | tf_op jit(solution)/shard_map/ppermute | solution.py:61
  22.3 9.3 %shard_map.75 = (f32[4,3,384,128]{3,2,1,0:T(8,128)S(1)}, f32[4,2,64,128]{3,2,1,0:T(8,128)S(1)}, f32[4,2,64,128]{3,2,1,0:T(8,128)S(1)}, f32[4,1,64,128]{3,2,1,0:T...) custom-call(s32[2,1,1,16]{3,2,1,0:T(1,128)S(1)} %copy-done, ...), custom_call_target="tpu_custom_call" | custom-call | tf_op jit(solution)/shard_map/pallas_call | solution.py:535
  31.7 3.6 %collective-permute-start.8 = (f32[4,2,64,128]{3,2,1,0:T(8,128)S(1)}, f32[4,2,64,128]{3,2,1,0:T(8,128)S(1)}, u32[]{:S(2)}, u32[]{:S(2)}) collective-permute-start(f32[4,2,64,128]{3,2,1,0:T(8,128)S(1)} %get-tuple-element.67), channel_id=1, source_target_pairs={{8,16},{16,8},{9,17},{17,9},{10,18},{18,10},{11,19},{19,11},{12,20... | collective-permute-start | bytes 786440 | tf_op jit(solution)/shard_map/ppermute | solution.py:61
  35.4 4.0 %collective-permute-done.8.row_odd = f32[4,2,64,128]{3,2,1,0:T(8,128)S(1)} collective-permute-done((f32[4,2,64,128]{3,2,1,0:T(8,128)S(1)}, f32[4,2,64,128]{3,2,1,0:T(8,128)S(1)}, u32[]{:S(2)}, u32[]{:S(2)}) %collective-permute-start.8) | collective-permute-done | bytes 262176 | tf_op jit(solution)/shard_map/ppermute | solution.py:61
  39.5 3.0 %collective-permute-start.10 = (f32[4,128,128]{2,1,0:T(8,128)S(1)}, f32[4,128,128]{2,1,0:T(8,128)S(1)}, u32[]{:S(2)}, u32[]{:S(2)}) collective-permute-start(f32[4,128,128]{2,1,0:T(8,128)S(1)} %get-tuple-element.70), channel_id=1, source_target_pairs={{1,2},{3,4},{5,6},{2,1},{4,3},{6,5},{9,10},{11,12},{13,14},{10,9},... | collective-permute-start | bytes 786440 | tf_op jit(solution)/shard_map/ppermute | solution.py:61
  42.6 3.9 %collective-permute-start.12 = (f32[4,1,64,128]{3,2,1,0:T(8,128)S(1)}, f32[4,1,64,128]{3,2,1,0:T(8,128)S(1)}, u32[]{:S(2)}, u32[]{:S(2)}) collective-permute-start(f32[4,1,64,128]{3,2,1,0:T(8,128)S(1)} %get-tuple-element.75), channel_id=1, source_target_pairs={{8,16},{16,8},{9,17},{17,9},{10,18},{18,10},{11,19},{19,11},{12,20... | collective-permute-start | bytes 393224 | tf_op jit(solution)/shard_map/ppermute | solution.py:61
  46.6 3.2 %collective-permute-start.14 = (f32[4,128,128]{2,1,0:T(8,128)S(1)}, f32[4,128,128]{2,1,0:T(8,128)S(1)}, u32[]{:S(2)}, u32[]{:S(2)}) collective-permute-start(f32[4,128,128]{2,1,0:T(8,128)S(1)} %get-tuple-element.82), channel_id=1, source_target_pairs={{1,2},{3,4},{5,6},{2,1},{4,3},{6,5},{9,10},{11,12},{13,14},{10,9},... | collective-permute-start | bytes 786440 | tf_op jit(solution)/shard_map/ppermute | solution.py:61
  50.9 3.9 %collective-permute-start.18 = (f32[4,1,64,128]{3,2,1,0:T(8,128)S(1)}, f32[4,1,64,128]{3,2,1,0:T(8,128)S(1)}, u32[]{:S(2)}, u32[]{:S(2)}) collective-permute-start(f32[4,1,64,128]{3,2,1,0:T(8,128)S(1)} %get-tuple-element.86), channel_id=1, source_target_pairs={{8,16},{16,8},{9,17},{17,9},{10,18},{18,10},{11,19},{19,11},{12,20... | collective-permute-start | bytes 393224 | tf_op jit(solution)/shard_map/ppermute | solution.py:61
  54.8 5.3 %collective-permute-done.11.from_even = f32[4,128,128]{2,1,0:T(8,128)S(1)} collective-permute-done((f32[4,128,128]{2,1,0:T(8,128)S(1)}, f32[4,128,128]{2,1,0:T(8,128)S(1)}, u32[]{:S(2)}, u32[]{:S(2)}) %collective-permute-start.11) | collective-permute-done | bytes 262176 | tf_op jit(solution)/shard_map/ppermute | solution.py:61
  60.2 2.6 %collective-permute-start.16 = (f32[4,2,64,128]{3,2,1,0:T(8,128)S(1)}, f32[4,2,64,128]{3,2,1,0:T(8,128)S(1)}, u32[]{:S(2)}, u32[]{:S(2)}) collective-permute-start(f32[4,2,64,128]{3,2,1,0:T(8,128)S(1)} %get-tuple-element.84), channel_id=1, source_target_pairs={{8,16},{16,8},{9,17},{17,9},{10,18},{18,10},{11,19},{19,11},{12,20... | collective-permute-start | bytes 786440 | tf_op jit(solution)/shard_map/ppermute | solution.py:61
  65.5 2.4 %collective-permute-done.16.row_odd = f32[4,2,64,128]{3,2,1,0:T(8,128)S(1)} collective-permute-done((f32[4,2,64,128]{3,2,1,0:T(8,128)S(1)}, f32[4,2,64,128]{3,2,1,0:T(8,128)S(1)}, u32[]{:S(2)}, u32[]{:S(2)}) %collective-permute-start.16) | collective-permute-done | bytes 262176 | tf_op jit(solution)/shard_map/ppermute | solution.py:61
  67.9 9.6 %shard_map.79 = (f32[4,3,384,128]{3,2,1,0:T(8,128)S(1)}, f32[4,3,64,128]{3,2,1,0:T(8,128)S(1)}, f32[4,3,64,128]{3,2,1,0:T(8,128)S(1)}, f32[4,3,128,128]{3,2,1,0:...) custom-call(s32[2,1,1,16]{3,2,1,0:T(1,128)S(1)} %copy-done, ...), custom_call_target="tpu_custom_call" | custom-call | tf_op jit(solution)/shard_map/pallas_call | solution.py:535
  77.5 2.6 %collective-permute-start.20 = (f32[4,3,64,128]{3,2,1,0:T(8,128)S(1)}, f32[4,3,64,128]{3,2,1,0:T(8,128)S(1)}, u32[]{:S(2)}, u32[]{:S(2)}) collective-permute-start(f32[4,3,64,128]{3,2,1,0:T(8,128)S(1)} %get-tuple-element.90), channel_id=1, source_target_pairs={{8,16},{16,8},{9,17},{17,9},{10,18},{18,10},{11,19},{19,11},{12,20... | collective-permute-start | bytes 1179656 | tf_op jit(solution)/shard_map/ppermute | solution.py:61
  80.1 2.8 %collective-permute-start.24 = (f32[4,64,128]{2,1,0:T(8,128)S(1)}, f32[4,64,128]{2,1,0:T(8,128)S(1)}, u32[]{:S(2)}, u32[]{:S(2)}) collective-permute-start(f32[4,64,128]{2,1,0:T(8,128)S(1)} %get-tuple-element.97), channel_id=1, source_target_pairs={{1,2},{3,4},{5,6},{2,1},{4,3},{6,5},{9,10},{11,12},{13,14},{10,9},... | collective-permute-start | bytes 393224 | tf_op jit(solution)/shard_map/ppermute | solution.py:61
  83.0 3.9 %collective-permute-done.20.row_odd = f32[4,3,64,128]{3,2,1,0:T(8,128)S(1)} collective-permute-done((f32[4,3,64,128]{3,2,1,0:T(8,128)S(1)}, f32[4,3,64,128]{3,2,1,0:T(8,128)S(1)}, u32[]{:S(2)}, u32[]{:S(2)}) %collective-permute-start.20) | collective-permute-done | bytes 393248 | tf_op jit(solution)/shard_map/ppermute | solution.py:61
  87.0 2.9 %collective-permute-start.22 = (f32[4,64,128]{2,1,0:T(8,128)S(1)}, f32[4,64,128]{2,1,0:T(8,128)S(1)}, u32[]{:S(2)}, u32[]{:S(2)}) collective-permute-start(f32[4,64,128]{2,1,0:T(8,128)S(1)} %get-tuple-element.92), channel_id=1, source_target_pairs={{1,2},{3,4},{5,6},{2,1},{4,3},{6,5},{9,10},{11,12},{13,14},{10,9},... | collective-permute-start | bytes 393224 | tf_op jit(solution)/shard_map/ppermute | solution.py:61
  90.0 2.5 %collective-permute-done.25.from_even = f32[4,64,128]{2,1,0:T(8,128)S(1)} collective-permute-done((f32[4,64,128]{2,1,0:T(8,128)S(1)}, f32[4,64,128]{2,1,0:T(8,128)S(1)}, u32[]{:S(2)}, u32[]{:S(2)}) %collective-permute-start.25) | collective-permute-done | bytes 131104 | tf_op jit(solution)/shard_map/ppermute | solution.py:61
  93.9 2.9 %collective-permute-done.23.from_even = f32[4,64,128]{2,1,0:T(8,128)S(1)} collective-permute-done((f32[4,64,128]{2,1,0:T(8,128)S(1)}, f32[4,64,128]{2,1,0:T(8,128)S(1)}, u32[]{:S(2)}, u32[]{:S(2)}) %collective-permute-start.23) | collective-permute-done | bytes 131104 | tf_op jit(solution)/shard_map/ppermute | solution.py:61
  (40 shorter events, 7.5 us)
Async XLA Ops:
  2.1 11.0 %collective-permute-start = (f32[4,64,128]{2,1,0:T(8,128)S(1)}, f32[4,64,128]{2,1,0:T(8,128)S(1)}, u32[]{:S(2)}, u32[]{:S(2)}) collective-permute-start(f32[4,64,128]{2,1,0:T(8,128)S(1)} %get-tuple-element.53), channel_id=1, source_target_pairs={{1,2},{3,4},{5,6},{2,1},{4,3},{6,5},{9,10},{11,12},{13,14},{10,9},... | collective-permute-start | bytes 393224 | tf_op jit(solution)/shard_map/ppermute | solution.py:61
  5.1 10.8 %collective-permute-start.1 = (f32[4,64,128]{2,1,0:T(8,128)S(1)}, f32[4,64,128]{2,1,0:T(8,128)S(1)}, u32[]{:S(2)}, u32[]{:S(2)}) collective-permute-start(f32[4,64,128]{2,1,0:T(8,128)S(1)} %get-tuple-element.54), channel_id=1, source_target_pairs={{0,1},{2,3},{4,5},{6,7},{1,0},{3,2},{5,4},{7,6},{8,9},{10,11},{12,... | collective-permute-start | bytes 393224 | tf_op jit(solution)/shard_map/ppermute | solution.py:61
  5.2 14.4 %collective-permute-start.2 = (f32[4,64,128]{2,1,0:T(8,128)S(1)}, f32[4,64,128]{2,1,0:T(8,128)S(1)}, u32[]{:S(2)}, u32[]{:S(2)}) collective-permute-start(f32[4,64,128]{2,1,0:T(8,128)S(1)} %get-tuple-element.55), channel_id=1, source_target_pairs={{1,2},{3,4},{5,6},{2,1},{4,3},{6,5},{9,10},{11,12},{13,14},{10,9},... | collective-permute-start | bytes 393224 | tf_op jit(solution)/shard_map/ppermute | solution.py:61
  8.5 13.9 %collective-permute-start.4 = (f32[4,2,64,128]{3,2,1,0:T(8,128)S(1)}, f32[4,2,64,128]{3,2,1,0:T(8,128)S(1)}, u32[]{:S(2)}, u32[]{:S(2)}) collective-permute-start(f32[4,2,64,128]{3,2,1,0:T(8,128)S(1)} %get-tuple-element.57), channel_id=1, source_target_pairs={{8,16},{16,8},{9,17},{17,9},{10,18},{18,10},{11,19},{19,11},{12,20... | collective-permute-start | bytes 786440 | tf_op jit(solution)/shard_map/ppermute | solution.py:61
  13.0 9.3 %collective-permute-start.5 = (f32[4,2,64,128]{3,2,1,0:T(8,128)S(1)}, f32[4,2,64,128]{3,2,1,0:T(8,128)S(1)}, u32[]{:S(2)}, u32[]{:S(2)}) collective-permute-start(f32[4,2,64,128]{3,2,1,0:T(8,128)S(1)} %get-tuple-element.58), channel_id=1, source_target_pairs={{0,8},{16,24},{8,0},{24,16},{1,9},{17,25},{9,1},{25,17},{2,10},{18... | collective-permute-start | bytes 786440 | tf_op jit(solution)/shard_map/ppermute | solution.py:61
  13.1 7.3 %collective-permute-start.3 = (f32[4,64,128]{2,1,0:T(8,128)S(1)}, f32[4,64,128]{2,1,0:T(8,128)S(1)}, u32[]{:S(2)}, u32[]{:S(2)}) collective-permute-start(f32[4,64,128]{2,1,0:T(8,128)S(1)} %get-tuple-element.56), channel_id=1, source_target_pairs={{0,1},{2,3},{4,5},{6,7},{1,0},{3,2},{5,4},{7,6},{8,9},{10,11},{12,... | collective-permute-start | bytes 393224 | tf_op jit(solution)/shard_map/ppermute | solution.py:61
  16.0 6.3 %collective-permute-start.6 = (f32[4,64,128]{2,1,0:T(8,128)S(1)}, f32[4,64,128]{2,1,0:T(8,128)S(1)}, u32[]{:S(2)}, u32[]{:S(2)}) collective-permute-start(f32[4,64,128]{2,1,0:T(8,128)S(1)} %get-tuple-element.59), channel_id=1, source_target_pairs={{8,16},{16,8},{9,17},{17,9},{10,18},{18,10},{11,19},{19,11},{12,20... | collective-permute-start | bytes 393224 | tf_op jit(solution)/shard_map/ppermute | solution.py:61
  31.7 7.7 %collective-permute-start.8 = (f32[4,2,64,128]{3,2,1,0:T(8,128)S(1)}, f32[4,2,64,128]{3,2,1,0:T(8,128)S(1)}, u32[]{:S(2)}, u32[]{:S(2)}) collective-permute-start(f32[4,2,64,128]{3,2,1,0:T(8,128)S(1)} %get-tuple-element.67), channel_id=1, source_target_pairs={{8,16},{16,8},{9,17},{17,9},{10,18},{18,10},{11,19},{19,11},{12,20... | collective-permute-start | bytes 786440 | tf_op jit(solution)/shard_map/ppermute | solution.py:61
  35.3 4.1 %collective-permute-start.9 = (f32[4,2,64,128]{3,2,1,0:T(8,128)S(1)}, f32[4,2,64,128]{3,2,1,0:T(8,128)S(1)}, u32[]{:S(2)}, u32[]{:S(2)}) collective-permute-start(f32[4,2,64,128]{3,2,1,0:T(8,128)S(1)} %get-tuple-element.68), channel_id=1, source_target_pairs={{0,8},{16,24},{8,0},{24,16},{1,9},{17,25},{9,1},{25,17},{2,10},{18... | collective-permute-start | bytes 786440 | tf_op jit(solution)/shard_map/ppermute | solution.py:61
  39.5 15.3 %collective-permute-start.10 = (f32[4,128,128]{2,1,0:T(8,128)S(1)}, f32[4,128,128]{2,1,0:T(8,128)S(1)}, u32[]{:S(2)}, u32[]{:S(2)}) collective-permute-start(f32[4,128,128]{2,1,0:T(8,128)S(1)} %get-tuple-element.70), channel_id=1, source_target_pairs={{1,2},{3,4},{5,6},{2,1},{4,3},{6,5},{9,10},{11,12},{13,14},{10,9},... | collective-permute-start | bytes 786440 | tf_op jit(solution)/shard_map/ppermute | solution.py:61
  42.5 17.6 %collective-permute-start.11 = (f32[4,128,128]{2,1,0:T(8,128)S(1)}, f32[4,128,128]{2,1,0:T(8,128)S(1)}, u32[]{:S(2)}, u32[]{:S(2)}) collective-permute-start(f32[4,128,128]{2,1,0:T(8,128)S(1)} %get-tuple-element.71), channel_id=1, source_target_pairs={{0,1},{2,3},{4,5},{6,7},{1,0},{3,2},{5,4},{7,6},{8,9},{10,11},{12,... | collective-permute-start | bytes 786440 | tf_op jit(solution)/shard_map/ppermute | solution.py:61
  42.6 7.2 %collective-permute-start.12 = (f32[4,1,64,128]{3,2,1,0:T(8,128)S(1)}, f32[4,1,64,128]{3,2,1,0:T(8,128)S(1)}, u32[]{:S(2)}, u32[]{:S(2)}) collective-permute-start(f32[4,1,64,128]{3,2,1,0:T(8,128)S(1)} %get-tuple-element.75), channel_id=1, source_target_pairs={{8,16},{16,8},{9,17},{17,9},{10,18},{18,10},{11,19},{19,11},{12,20... | collective-permute-start | bytes 393224 | tf_op jit(solution)/shard_map/ppermute | solution.py:61
  46.5 4.4 %collective-permute-start.13 = (f32[4,1,64,128]{3,2,1,0:T(8,128)S(1)}, f32[4,1,64,128]{3,2,1,0:T(8,128)S(1)}, u32[]{:S(2)}, u32[]{:S(2)}) collective-permute-start(f32[4,1,64,128]{3,2,1,0:T(8,128)S(1)} %get-tuple-element.76), channel_id=1, source_target_pairs={{0,8},{16,24},{8,0},{24,16},{1,9},{17,25},{9,1},{25,17},{2,10},{18... | collective-permute-start | bytes 393224 | tf_op jit(solution)/shard_map/ppermute | solution.py:61
  46.6 18.0 %collective-permute-start.14 = (f32[4,128,128]{2,1,0:T(8,128)S(1)}, f32[4,128,128]{2,1,0:T(8,128)S(1)}, u32[]{:S(2)}, u32[]{:S(2)}) collective-permute-start(f32[4,128,128]{2,1,0:T(8,128)S(1)} %get-tuple-element.82), channel_id=1, source_target_pairs={{1,2},{3,4},{5,6},{2,1},{4,3},{6,5},{9,10},{11,12},{13,14},{10,9},... | collective-permute-start | bytes 786440 | tf_op jit(solution)/shard_map/ppermute | solution.py:61
  49.8 15.7 %collective-permute-start.15 = (f32[4,128,128]{2,1,0:T(8,128)S(1)}, f32[4,128,128]{2,1,0:T(8,128)S(1)}, u32[]{:S(2)}, u32[]{:S(2)}) collective-permute-start(f32[4,128,128]{2,1,0:T(8,128)S(1)} %get-tuple-element.83), channel_id=1, source_target_pairs={{0,1},{2,3},{4,5},{6,7},{1,0},{3,2},{5,4},{7,6},{8,9},{10,11},{12,... | collective-permute-start | bytes 786440 | tf_op jit(solution)/shard_map/ppermute | solution.py:61
  50.9 11.9 %collective-permute-start.18 = (f32[4,1,64,128]{3,2,1,0:T(8,128)S(1)}, f32[4,1,64,128]{3,2,1,0:T(8,128)S(1)}, u32[]{:S(2)}, u32[]{:S(2)}) collective-permute-start(f32[4,1,64,128]{3,2,1,0:T(8,128)S(1)} %get-tuple-element.86), channel_id=1, source_target_pairs={{8,16},{16,8},{9,17},{17,9},{10,18},{18,10},{11,19},{19,11},{12,20... | collective-permute-start | bytes 393224 | tf_op jit(solution)/shard_map/ppermute | solution.py:61
  60.2 7.7 %collective-permute-start.16 = (f32[4,2,64,128]{3,2,1,0:T(8,128)S(1)}, f32[4,2,64,128]{3,2,1,0:T(8,128)S(1)}, u32[]{:S(2)}, u32[]{:S(2)}) collective-permute-start(f32[4,2,64,128]{3,2,1,0:T(8,128)S(1)} %get-tuple-element.84), channel_id=1, source_target_pairs={{8,16},{16,8},{9,17},{17,9},{10,18},{18,10},{11,19},{19,11},{12,20... | collective-permute-start | bytes 786440 | tf_op jit(solution)/shard_map/ppermute | solution.py:61
  62.8 5.1 %collective-permute-start.17 = (f32[4,2,64,128]{3,2,1,0:T(8,128)S(1)}, f32[4,2,64,128]{3,2,1,0:T(8,128)S(1)}, u32[]{:S(2)}, u32[]{:S(2)}) collective-permute-start(f32[4,2,64,128]{3,2,1,0:T(8,128)S(1)} %get-tuple-element.85), channel_id=1, source_target_pairs={{0,8},{16,24},{8,0},{24,16},{1,9},{17,25},{9,1},{25,17},{2,10},{18... | collective-permute-start | bytes 786440 | tf_op jit(solution)/shard_map/ppermute | solution.py:61
  77.5 9.4 %collective-permute-start.20 = (f32[4,3,64,128]{3,2,1,0:T(8,128)S(1)}, f32[4,3,64,128]{3,2,1,0:T(8,128)S(1)}, u32[]{:S(2)}, u32[]{:S(2)}) collective-permute-start(f32[4,3,64,128]{3,2,1,0:T(8,128)S(1)} %get-tuple-element.90), channel_id=1, source_target_pairs={{8,16},{16,8},{9,17},{17,9},{10,18},{18,10},{11,19},{19,11},{12,20... | collective-permute-start | bytes 1179656 | tf_op jit(solution)/shard_map/ppermute | solution.py:61
  80.0 6.8 %collective-permute-start.21 = (f32[4,3,64,128]{3,2,1,0:T(8,128)S(1)}, f32[4,3,64,128]{3,2,1,0:T(8,128)S(1)}, u32[]{:S(2)}, u32[]{:S(2)}) collective-permute-start(f32[4,3,64,128]{3,2,1,0:T(8,128)S(1)} %get-tuple-element.91), channel_id=1, source_target_pairs={{0,8},{16,24},{8,0},{24,16},{1,9},{17,25},{9,1},{25,17},{2,10},{18... | collective-permute-start | bytes 1179656 | tf_op jit(solution)/shard_map/ppermute | solution.py:61
  80.1 9.9 %collective-permute-start.24 = (f32[4,64,128]{2,1,0:T(8,128)S(1)}, f32[4,64,128]{2,1,0:T(8,128)S(1)}, u32[]{:S(2)}, u32[]{:S(2)}) collective-permute-start(f32[4,64,128]{2,1,0:T(8,128)S(1)} %get-tuple-element.97), channel_id=1, source_target_pairs={{1,2},{3,4},{5,6},{2,1},{4,3},{6,5},{9,10},{11,12},{13,14},{10,9},... | collective-permute-start | bytes 393224 | tf_op jit(solution)/shard_map/ppermute | solution.py:61
  82.9 9.6 %collective-permute-start.25 = (f32[4,64,128]{2,1,0:T(8,128)S(1)}, f32[4,64,128]{2,1,0:T(8,128)S(1)}, u32[]{:S(2)}, u32[]{:S(2)}) collective-permute-start(f32[4,64,128]{2,1,0:T(8,128)S(1)} %get-tuple-element.98), channel_id=1, source_target_pairs={{0,1},{2,3},{4,5},{6,7},{1,0},{3,2},{5,4},{7,6},{8,9},{10,11},{12,... | collective-permute-start | bytes 393224 | tf_op jit(solution)/shard_map/ppermute | solution.py:61
  87.0 6.9 %collective-permute-start.22 = (f32[4,64,128]{2,1,0:T(8,128)S(1)}, f32[4,64,128]{2,1,0:T(8,128)S(1)}, u32[]{:S(2)}, u32[]{:S(2)}) collective-permute-start(f32[4,64,128]{2,1,0:T(8,128)S(1)} %get-tuple-element.92), channel_id=1, source_target_pairs={{1,2},{3,4},{5,6},{2,1},{4,3},{6,5},{9,10},{11,12},{13,14},{10,9},... | collective-permute-start | bytes 393224 | tf_op jit(solution)/shard_map/ppermute | solution.py:61
  89.9 6.9 %collective-permute-start.23 = (f32[4,64,128]{2,1,0:T(8,128)S(1)}, f32[4,64,128]{2,1,0:T(8,128)S(1)}, u32[]{:S(2)}, u32[]{:S(2)}) collective-permute-start(f32[4,64,128]{2,1,0:T(8,128)S(1)} %get-tuple-element.93), channel_id=1, source_target_pairs={{0,1},{2,3},{4,5},{6,7},{1,0},{3,2},{5,4},{7,6},{8,9},{10,11},{12,... | collective-permute-start | bytes 393224 | tf_op jit(solution)/shard_map/ppermute | solution.py:61
  (3 other events, 26.7 us)
where the time goes:
time: 98.5 us; the launch traced here: 98 us
  starting transfers between devices  45.2 us (46%)
  waiting for transfers between devices  27.8 us (28%)
  Pallas kernels  24 us (24%)
  between operations  0.99 us (1%)
    ppermute x26, starting transfers between devices, exchange(): received.append(lax.ppermute(values, axis, pairs))  45.2 us
    ppermute x26, waiting for transfers between devices, exchange(): received.append(lax.ppermute(values, axis, pairs))  27.8 us
    pallas_call x10, Pallas kernels, run(): pl.pallas_call(kernel, out_shape=outs, input_output_aliases=alias or {},...  24 us
  transfers between devices with their start and end apart: 26, of which 10 were waited for; matrix products, arithmetic and copies ran while one was open for 0% of the time, Pallas kernels for 2%

commit v1 on v0

--- a/solution.py
+++ b/solution.py
@@ -12,6 +12,7 @@
 ITERS = 2
 LANES = 128
 GROUP = 8
+BATCH = 4
 
 modulus_offset = 0.5
 fresnel_scale = 0.9
@@ -170,7 +171,8 @@
     def right(source, kind):
         table_high, table_low = rights_ref[2 * kind], rights_ref[2 * kind + 1]
         high, low = split(source)
-        return dot(high, table_high) + (dot(low, table_high) + dot(high, table_low))
+        out = dot(jnp.concatenate([high, low], axis=0), table_high)
+        return out[: high.shape[0]] + out[high.shape[0] :] + dot(high, table_low)
 
     def left(re, im, kind):
         upper, lower = (re[:half], im[:half]), (re[half:], im[half:])
@@ -195,13 +197,11 @@
         return [jnp.concatenate([a, b], axis=0) for a, b in zip(upper, lower)]
 
     def two_sided(zs, kind):
-        outs = [
-            right(
-                jnp.concatenate([jnp.concatenate(z, axis=1) for z in zs[pair : pair + 2]], axis=0),
-                kind,
-            )
-            for pair in range(0, len(zs), 2)
-        ]
+        outs = []
+        for first in range(0, len(zs), BATCH):
+            rows = [jnp.concatenate(z, axis=1) for z in zs[first : first + BATCH]]
+            out = right(jnp.concatenate(rows, axis=0), kind)
+            outs.extend(out[at : at + 2 * frame] for at in range(0, BATCH * frame, 2 * frame))
         mixes = [
             left(
                 jnp.concatenate([out[:frame, :frame], out[frame:, :frame]], axis=1),

time: 98.5 us -> 98.9 us (level)
  no operation moved by 1% of the time
where the time goes in v1:
time: 98.9 us; the launch traced here: 98.5 us
  starting transfers between devices  45.3 us (46%)
  waiting for transfers between devices  27.7 us (28%)
  Pallas kernels  24.5 us (25%)
  between operations  0.99 us (1%)
    ppermute x26, starting transfers between devices, exchange(): received.append(lax.ppermute(values, axis, pairs))  45.3 us
    ppermute x26, waiting for transfers between devices, exchange(): received.append(lax.ppermute(values, axis, pairs))  27.7 us
    pallas_call x10, Pallas kernels, run(): pl.pallas_call(kernel, out_shape=outs, input_output_aliases=alias or {},...  24.5 us
  transfers between devices with their start and end apart: 26, of which 10 were waited for; matrix products, arithmetic and copies ran while one was open for 0% of the time, Pallas kernels for 2%

profile of v1, /device:TPU:25, one launch (start us, length us, event | category | flops | bytes accessed | tf_op | source)
XLA Modules:
  0.0 98.5 jit_solution(1451690919826701409)
XLA Ops:
  0.0 2.1 %shard_map.73 = (f32[4,2,256,128]{3,2,1,0:T(8,128)S(1)}, f32[4,64,128]{2,1,0:T(8,128)S(1)}, f32[4,64,128]{2,1,0:T(8,128)S(1)}, f32[4,64,128]{2,1,0:T(8,128)S(1)}...) custom-call(f32[4,256,256]{2,1,0:T(8,128)} %bitcast.3, ...), custom_call_target="tpu_custom_call" | custom-call | tf_op jit(solution)/shard_map/pallas_call | solution.py:535
  2.1 3.0 %collective-permute-start = (f32[4,64,128]{2,1,0:T(8,128)S(1)}, f32[4,64,128]{2,1,0:T(8,128)S(1)}, u32[]{:S(2)}, u32[]{:S(2)}) collective-permute-start(f32[4,64,128]{2,1,0:T(8,128)S(1)} %get-tuple-element.53), channel_id=1, source_target_pairs={{1,2},{3,4},{5,6},{2,1},{4,3},{6,5},{9,10},{11,12},{13,14},{10,9},... | collective-permute-start | bytes 393224 | tf_op jit(solution)/shard_map/ppermute | solution.py:62
  5.2 3.2 %collective-permute-start.2 = (f32[4,64,128]{2,1,0:T(8,128)S(1)}, f32[4,64,128]{2,1,0:T(8,128)S(1)}, u32[]{:S(2)}, u32[]{:S(2)}) collective-permute-start(f32[4,64,128]{2,1,0:T(8,128)S(1)} %get-tuple-element.55), channel_id=1, source_target_pairs={{1,2},{3,4},{5,6},{2,1},{4,3},{6,5},{9,10},{11,12},{13,14},{10,9},... | collective-permute-start | bytes 393224 | tf_op jit(solution)/shard_map/ppermute | solution.py:62
  8.5 4.5 %collective-permute-start.4 = (f32[4,2,64,128]{3,2,1,0:T(8,128)S(1)}, f32[4,2,64,128]{3,2,1,0:T(8,128)S(1)}, u32[]{:S(2)}, u32[]{:S(2)}) collective-permute-start(f32[4,2,64,128]{3,2,1,0:T(8,128)S(1)} %get-tuple-element.57), channel_id=1, source_target_pairs={{8,16},{16,8},{9,17},{17,9},{10,18},{18,10},{11,19},{19,11},{12,20... | collective-permute-start | bytes 786440 | tf_op jit(solution)/shard_map/ppermute | solution.py:62
  13.2 2.8 %collective-permute-done.1.from_even.edge_even = f32[4,64,128]{2,1,0:T(8,128)S(1)} collective-permute-done((f32[4,64,128]{2,1,0:T(8,128)S(1)}, f32[4,64,128]{2,1,0:T(8,128)S(1)}, u32[]{:S(2)}, u32[]{:S(2)}) %collective-permute-start.1) | collective-permute-done | bytes 131104 | tf_op jit(solution)/shard_map/ppermute | solution.py:62
  16.0 3.6 %collective-permute-start.6 = (f32[4,64,128]{2,1,0:T(8,128)S(1)}, f32[4,64,128]{2,1,0:T(8,128)S(1)}, u32[]{:S(2)}, u32[]{:S(2)}) collective-permute-start(f32[4,64,128]{2,1,0:T(8,128)S(1)} %get-tuple-element.59), channel_id=1, source_target_pairs={{8,16},{16,8},{9,17},{17,9},{10,18},{18,10},{11,19},{19,11},{12,20... | collective-permute-start | bytes 393224 | tf_op jit(solution)/shard_map/ppermute | solution.py:62
  20.4 1.9 %collective-permute-done.6.corner_odd = f32[4,64,128]{2,1,0:T(8,128)S(1)} collective-permute-done((f32[4,64,128]{2,1,0:T(8,128)S(1)}, f32[4,64,128]{2,1,0:T(8,128)S(1)}, u32[]{:S(2)}, u32[]{:S(2)}) %collective-permute-start.6) | collective-permute-done | bytes 131104 | tf_op jit(solution)/shard_map/ppermute | solution.py:62
  22.3 9.6 %shard_map.75 = (f32[4,3,384,128]{3,2,1,0:T(8,128)S(1)}, f32[4,2,64,128]{3,2,1,0:T(8,128)S(1)}, f32[4,2,64,128]{3,2,1,0:T(8,128)S(1)}, f32[4,1,64,128]{3,2,1,0:T...) custom-call(s32[2,1,1,16]{3,2,1,0:T(1,128)S(1)} %copy-done, ...), custom_call_target="tpu_custom_call" | custom-call | tf_op jit(solution)/shard_map/pallas_call | solution.py:535
  31.9 3.6 %collective-permute-start.8 = (f32[4,2,64,128]{3,2,1,0:T(8,128)S(1)}, f32[4,2,64,128]{3,2,1,0:T(8,128)S(1)}, u32[]{:S(2)}, u32[]{:S(2)}) collective-permute-start(f32[4,2,64,128]{3,2,1,0:T(8,128)S(1)} %get-tuple-element.67), channel_id=1, source_target_pairs={{8,16},{16,8},{9,17},{17,9},{10,18},{18,10},{11,19},{19,11},{12,20... | collective-permute-start | bytes 786440 | tf_op jit(solution)/shard_map/ppermute | solution.py:62
  35.6 4.0 %collective-permute-done.8.row_odd = f32[4,2,64,128]{3,2,1,0:T(8,128)S(1)} collective-permute-done((f32[4,2,64,128]{3,2,1,0:T(8,128)S(1)}, f32[4,2,64,128]{3,2,1,0:T(8,128)S(1)}, u32[]{:S(2)}, u32[]{:S(2)}) %collective-permute-start.8) | collective-permute-done | bytes 262176 | tf_op jit(solution)/shard_map/ppermute | solution.py:62
  39.8 3.0 %collective-permute-start.10 = (f32[4,128,128]{2,1,0:T(8,128)S(1)}, f32[4,128,128]{2,1,0:T(8,128)S(1)}, u32[]{:S(2)}, u32[]{:S(2)}) collective-permute-start(f32[4,128,128]{2,1,0:T(8,128)S(1)} %get-tuple-element.70), channel_id=1, source_target_pairs={{1,2},{3,4},{5,6},{2,1},{4,3},{6,5},{9,10},{11,12},{13,14},{10,9},... | collective-permute-start | bytes 786440 | tf_op jit(solution)/shard_map/ppermute | solution.py:62
  42.9 3.9 %collective-permute-start.12 = (f32[4,1,64,128]{3,2,1,0:T(8,128)S(1)}, f32[4,1,64,128]{3,2,1,0:T(8,128)S(1)}, u32[]{:S(2)}, u32[]{:S(2)}) collective-permute-start(f32[4,1,64,128]{3,2,1,0:T(8,128)S(1)} %get-tuple-element.75), channel_id=1, source_target_pairs={{8,16},{16,8},{9,17},{17,9},{10,18},{18,10},{11,19},{19,11},{12,20... | collective-permute-start | bytes 393224 | tf_op jit(solution)/shard_map/ppermute | solution.py:62
  46.8 3.2 %collective-permute-start.14 = (f32[4,128,128]{2,1,0:T(8,128)S(1)}, f32[4,128,128]{2,1,0:T(8,128)S(1)}, u32[]{:S(2)}, u32[]{:S(2)}) collective-permute-start(f32[4,128,128]{2,1,0:T(8,128)S(1)} %get-tuple-element.82), channel_id=1, source_target_pairs={{1,2},{3,4},{5,6},{2,1},{4,3},{6,5},{9,10},{11,12},{13,14},{10,9},... | collective-permute-start | bytes 786440 | tf_op jit(solution)/shard_map/ppermute | solution.py:62
  51.2 3.9 %collective-permute-start.18 = (f32[4,1,64,128]{3,2,1,0:T(8,128)S(1)}, f32[4,1,64,128]{3,2,1,0:T(8,128)S(1)}, u32[]{:S(2)}, u32[]{:S(2)}) collective-permute-start(f32[4,1,64,128]{3,2,1,0:T(8,128)S(1)} %get-tuple-element.86), channel_id=1, source_target_pairs={{8,16},{16,8},{9,17},{17,9},{10,18},{18,10},{11,19},{19,11},{12,20... | collective-permute-start | bytes 393224 | tf_op jit(solution)/shard_map/ppermute | solution.py:62
  55.1 5.2 %collective-permute-done.11.from_even = f32[4,128,128]{2,1,0:T(8,128)S(1)} collective-permute-done((f32[4,128,128]{2,1,0:T(8,128)S(1)}, f32[4,128,128]{2,1,0:T(8,128)S(1)}, u32[]{:S(2)}, u32[]{:S(2)}) %collective-permute-start.11) | collective-permute-done | bytes 262176 | tf_op jit(solution)/shard_map/ppermute | solution.py:62
  60.4 2.6 %collective-permute-start.16 = (f32[4,2,64,128]{3,2,1,0:T(8,128)S(1)}, f32[4,2,64,128]{3,2,1,0:T(8,128)S(1)}, u32[]{:S(2)}, u32[]{:S(2)}) collective-permute-start(f32[4,2,64,128]{3,2,1,0:T(8,128)S(1)} %get-tuple-element.84), channel_id=1, source_target_pairs={{8,16},{16,8},{9,17},{17,9},{10,18},{18,10},{11,19},{19,11},{12,20... | collective-permute-start | bytes 786440 | tf_op jit(solution)/shard_map/ppermute | solution.py:62
  65.7 2.4 %collective-permute-done.16.row_odd = f32[4,2,64,128]{3,2,1,0:T(8,128)S(1)} collective-permute-done((f32[4,2,64,128]{3,2,1,0:T(8,128)S(1)}, f32[4,2,64,128]{3,2,1,0:T(8,128)S(1)}, u32[]{:S(2)}, u32[]{:S(2)}) %collective-permute-start.16) | collective-permute-done | bytes 262176 | tf_op jit(solution)/shard_map/ppermute | solution.py:62
  68.1 9.8 %shard_map.79 = (f32[4,3,384,128]{3,2,1,0:T(8,128)S(1)}, f32[4,3,64,128]{3,2,1,0:T(8,128)S(1)}, f32[4,3,64,128]{3,2,1,0:T(8,128)S(1)}, f32[4,3,128,128]{3,2,1,0:...) custom-call(s32[2,1,1,16]{3,2,1,0:T(1,128)S(1)} %copy-done, ...), custom_call_target="tpu_custom_call" | custom-call | tf_op jit(solution)/shard_map/pallas_call | solution.py:535
  77.9 2.6 %collective-permute-start.20 = (f32[4,3,64,128]{3,2,1,0:T(8,128)S(1)}, f32[4,3,64,128]{3,2,1,0:T(8,128)S(1)}, u32[]{:S(2)}, u32[]{:S(2)}) collective-permute-start(f32[4,3,64,128]{3,2,1,0:T(8,128)S(1)} %get-tuple-element.90), channel_id=1, source_target_pairs={{8,16},{16,8},{9,17},{17,9},{10,18},{18,10},{11,19},{19,11},{12,20... | collective-permute-start | bytes 1179656 | tf_op jit(solution)/shard_map/ppermute | solution.py:62
  80.6 2.8 %collective-permute-start.24 = (f32[4,64,128]{2,1,0:T(8,128)S(1)}, f32[4,64,128]{2,1,0:T(8,128)S(1)}, u32[]{:S(2)}, u32[]{:S(2)}) collective-permute-start(f32[4,64,128]{2,1,0:T(8,128)S(1)} %get-tuple-element.97), channel_id=1, source_target_pairs={{1,2},{3,4},{5,6},{2,1},{4,3},{6,5},{9,10},{11,12},{13,14},{10,9},... | collective-permute-start | bytes 393224 | tf_op jit(solution)/shard_map/ppermute | solution.py:62
  83.5 3.8 %collective-permute-done.20.row_odd = f32[4,3,64,128]{3,2,1,0:T(8,128)S(1)} collective-permute-done((f32[4,3,64,128]{3,2,1,0:T(8,128)S(1)}, f32[4,3,64,128]{3,2,1,0:T(8,128)S(1)}, u32[]{:S(2)}, u32[]{:S(2)}) %collective-permute-start.20) | collective-permute-done | bytes 393248 | tf_op jit(solution)/shard_map/ppermute | solution.py:62
  87.4 3.0 %collective-permute-start.22 = (f32[4,64,128]{2,1,0:T(8,128)S(1)}, f32[4,64,128]{2,1,0:T(8,128)S(1)}, u32[]{:S(2)}, u32[]{:S(2)}) collective-permute-start(f32[4,64,128]{2,1,0:T(8,128)S(1)} %get-tuple-element.92), channel_id=1, source_target_pairs={{1,2},{3,4},{5,6},{2,1},{4,3},{6,5},{9,10},{11,12},{13,14},{10,9},... | collective-permute-start | bytes 393224 | tf_op jit(solution)/shard_map/ppermute | solution.py:62
  90.5 2.5 %collective-permute-done.25.from_even = f32[4,64,128]{2,1,0:T(8,128)S(1)} collective-permute-done((f32[4,64,128]{2,1,0:T(8,128)S(1)}, f32[4,64,128]{2,1,0:T(8,128)S(1)}, u32[]{:S(2)}, u32[]{:S(2)}) %collective-permute-start.25) | collective-permute-done | bytes 131104 | tf_op jit(solution)/shard_map/ppermute | solution.py:62
  94.3 2.9 %collective-permute-done.23.from_even = f32[4,64,128]{2,1,0:T(8,128)S(1)} collective-permute-done((f32[4,64,128]{2,1,0:T(8,128)S(1)}, f32[4,64,128]{2,1,0:T(8,128)S(1)}, u32[]{:S(2)}, u32[]{:S(2)}) %collective-permute-start.23) | collective-permute-done | bytes 131104 | tf_op jit(solution)/shard_map/ppermute | solution.py:62
  (40 shorter events, 7.6 us)
Async XLA Ops:
  2.1 11.0 %collective-permute-start = (f32[4,64,128]{2,1,0:T(8,128)S(1)}, f32[4,64,128]{2,1,0:T(8,128)S(1)}, u32[]{:S(2)}, u32[]{:S(2)}) collective-permute-start(f32[4,64,128]{2,1,0:T(8,128)S(1)} %get-tuple-element.53), channel_id=1, source_target_pairs={{1,2},{3,4},{5,6},{2,1},{4,3},{6,5},{9,10},{11,12},{13,14},{10,9},... | collective-permute-start | bytes 393224 | tf_op jit(solution)/shard_map/ppermute | solution.py:62
  5.1 10.8 %collective-permute-start.1 = (f32[4,64,128]{2,1,0:T(8,128)S(1)}, f32[4,64,128]{2,1,0:T(8,128)S(1)}, u32[]{:S(2)}, u32[]{:S(2)}) collective-permute-start(f32[4,64,128]{2,1,0:T(8,128)S(1)} %get-tuple-element.54), channel_id=1, source_target_pairs={{0,1},{2,3},{4,5},{6,7},{1,0},{3,2},{5,4},{7,6},{8,9},{10,11},{12,... | collective-permute-start | bytes 393224 | tf_op jit(solution)/shard_map/ppermute | solution.py:62
  5.2 14.4 %collective-permute-start.2 = (f32[4,64,128]{2,1,0:T(8,128)S(1)}, f32[4,64,128]{2,1,0:T(8,128)S(1)}, u32[]{:S(2)}, u32[]{:S(2)}) collective-permute-start(f32[4,64,128]{2,1,0:T(8,128)S(1)} %get-tuple-element.55), channel_id=1, source_target_pairs={{1,2},{3,4},{5,6},{2,1},{4,3},{6,5},{9,10},{11,12},{13,14},{10,9},... | collective-permute-start | bytes 393224 | tf_op jit(solution)/shard_map/ppermute | solution.py:62
  8.5 13.9 %collective-permute-start.4 = (f32[4,2,64,128]{3,2,1,0:T(8,128)S(1)}, f32[4,2,64,128]{3,2,1,0:T(8,128)S(1)}, u32[]{:S(2)}, u32[]{:S(2)}) collective-permute-start(f32[4,2,64,128]{3,2,1,0:T(8,128)S(1)} %get-tuple-element.57), channel_id=1, source_target_pairs={{8,16},{16,8},{9,17},{17,9},{10,18},{18,10},{11,19},{19,11},{12,20... | collective-permute-start | bytes 786440 | tf_op jit(solution)/shard_map/ppermute | solution.py:62
  13.0 9.3 %collective-permute-start.5 = (f32[4,2,64,128]{3,2,1,0:T(8,128)S(1)}, f32[4,2,64,128]{3,2,1,0:T(8,128)S(1)}, u32[]{:S(2)}, u32[]{:S(2)}) collective-permute-start(f32[4,2,64,128]{3,2,1,0:T(8,128)S(1)} %get-tuple-element.58), channel_id=1, source_target_pairs={{0,8},{16,24},{8,0},{24,16},{1,9},{17,25},{9,1},{25,17},{2,10},{18... | collective-permute-start | bytes 786440 | tf_op jit(solution)/shard_map/ppermute | solution.py:62
  13.1 7.3 %collective-permute-start.3 = (f32[4,64,128]{2,1,0:T(8,128)S(1)}, f32[4,64,128]{2,1,0:T(8,128)S(1)}, u32[]{:S(2)}, u32[]{:S(2)}) collective-permute-start(f32[4,64,128]{2,1,0:T(8,128)S(1)} %get-tuple-element.56), channel_id=1, source_target_pairs={{0,1},{2,3},{4,5},{6,7},{1,0},{3,2},{5,4},{7,6},{8,9},{10,11},{12,... | collective-permute-start | bytes 393224 | tf_op jit(solution)/shard_map/ppermute | solution.py:62
  16.0 6.3 %collective-permute-start.6 = (f32[4,64,128]{2,1,0:T(8,128)S(1)}, f32[4,64,128]{2,1,0:T(8,128)S(1)}, u32[]{:S(2)}, u32[]{:S(2)}) collective-permute-start(f32[4,64,128]{2,1,0:T(8,128)S(1)} %get-tuple-element.59), channel_id=1, source_target_pairs={{8,16},{16,8},{9,17},{17,9},{10,18},{18,10},{11,19},{19,11},{12,20... | collective-permute-start | bytes 393224 | tf_op jit(solution)/shard_map/ppermute | solution.py:62
  31.9 7.7 %collective-permute-start.8 = (f32[4,2,64,128]{3,2,1,0:T(8,128)S(1)}, f32[4,2,64,128]{3,2,1,0:T(8,128)S(1)}, u32[]{:S(2)}, u32[]{:S(2)}) collective-permute-start(f32[4,2,64,128]{3,2,1,0:T(8,128)S(1)} %get-tuple-element.67), channel_id=1, source_target_pairs={{8,16},{16,8},{9,17},{17,9},{10,18},{18,10},{11,19},{19,11},{12,20... | collective-permute-start | bytes 786440 | tf_op jit(solution)/shard_map/ppermute | solution.py:62
  35.6 4.1 %collective-permute-start.9 = (f32[4,2,64,128]{3,2,1,0:T(8,128)S(1)}, f32[4,2,64,128]{3,2,1,0:T(8,128)S(1)}, u32[]{:S(2)}, u32[]{:S(2)}) collective-permute-start(f32[4,2,64,128]{3,2,1,0:T(8,128)S(1)} %get-tuple-element.68), channel_id=1, source_target_pairs={{0,8},{16,24},{8,0},{24,16},{1,9},{17,25},{9,1},{25,17},{2,10},{18... | collective-permute-start | bytes 786440 | tf_op jit(solution)/shard_map/ppermute | solution.py:62
  39.8 15.3 %collective-permute-start.10 = (f32[4,128,128]{2,1,0:T(8,128)S(1)}, f32[4,128,128]{2,1,0:T(8,128)S(1)}, u32[]{:S(2)}, u32[]{:S(2)}) collective-permute-start(f32[4,128,128]{2,1,0:T(8,128)S(1)} %get-tuple-element.70), channel_id=1, source_target_pairs={{1,2},{3,4},{5,6},{2,1},{4,3},{6,5},{9,10},{11,12},{13,14},{10,9},... | collective-permute-start | bytes 786440 | tf_op jit(solution)/shard_map/ppermute | solution.py:62
  42.8 17.5 %collective-permute-start.11 = (f32[4,128,128]{2,1,0:T(8,128)S(1)}, f32[4,128,128]{2,1,0:T(8,128)S(1)}, u32[]{:S(2)}, u32[]{:S(2)}) collective-permute-start(f32[4,128,128]{2,1,0:T(8,128)S(1)} %get-tuple-element.71), channel_id=1, source_target_pairs={{0,1},{2,3},{4,5},{6,7},{1,0},{3,2},{5,4},{7,6},{8,9},{10,11},{12,... | collective-permute-start | bytes 786440 | tf_op jit(solution)/shard_map/ppermute | solution.py:62
  42.9 7.1 %collective-permute-start.12 = (f32[4,1,64,128]{3,2,1,0:T(8,128)S(1)}, f32[4,1,64,128]{3,2,1,0:T(8,128)S(1)}, u32[]{:S(2)}, u32[]{:S(2)}) collective-permute-start(f32[4,1,64,128]{3,2,1,0:T(8,128)S(1)} %get-tuple-element.75), channel_id=1, source_target_pairs={{8,16},{16,8},{9,17},{17,9},{10,18},{18,10},{11,19},{19,11},{12,20... | collective-permute-start | bytes 393224 | tf_op jit(solution)/shard_map/ppermute | solution.py:62
  46.7 4.4 %collective-permute-start.13 = (f32[4,1,64,128]{3,2,1,0:T(8,128)S(1)}, f32[4,1,64,128]{3,2,1,0:T(8,128)S(1)}, u32[]{:S(2)}, u32[]{:S(2)}) collective-permute-start(f32[4,1,64,128]{3,2,1,0:T(8,128)S(1)} %get-tuple-element.76), channel_id=1, source_target_pairs={{0,8},{16,24},{8,0},{24,16},{1,9},{17,25},{9,1},{25,17},{2,10},{18... | collective-permute-start | bytes 393224 | tf_op jit(solution)/shard_map/ppermute | solution.py:62
  46.8 18.0 %collective-permute-start.14 = (f32[4,128,128]{2,1,0:T(8,128)S(1)}, f32[4,128,128]{2,1,0:T(8,128)S(1)}, u32[]{:S(2)}, u32[]{:S(2)}) collective-permute-start(f32[4,128,128]{2,1,0:T(8,128)S(1)} %get-tuple-element.82), channel_id=1, source_target_pairs={{1,2},{3,4},{5,6},{2,1},{4,3},{6,5},{9,10},{11,12},{13,14},{10,9},... | collective-permute-start | bytes 786440 | tf_op jit(solution)/shard_map/ppermute | solution.py:62
  50.0 15.7 %collective-permute-start.15 = (f32[4,128,128]{2,1,0:T(8,128)S(1)}, f32[4,128,128]{2,1,0:T(8,128)S(1)}, u32[]{:S(2)}, u32[]{:S(2)}) collective-permute-start(f32[4,128,128]{2,1,0:T(8,128)S(1)} %get-tuple-element.83), channel_id=1, source_target_pairs={{0,1},{2,3},{4,5},{6,7},{1,0},{3,2},{5,4},{7,6},{8,9},{10,11},{12,... | collective-permute-start | bytes 786440 | tf_op jit(solution)/shard_map/ppermute | solution.py:62
  51.2 11.9 %collective-permute-start.18 = (f32[4,1,64,128]{3,2,1,0:T(8,128)S(1)}, f32[4,1,64,128]{3,2,1,0:T(8,128)S(1)}, u32[]{:S(2)}, u32[]{:S(2)}) collective-permute-start(f32[4,1,64,128]{3,2,1,0:T(8,128)S(1)} %get-tuple-element.86), channel_id=1, source_target_pairs={{8,16},{16,8},{9,17},{17,9},{10,18},{18,10},{11,19},{19,11},{12,20... | collective-permute-start | bytes 393224 | tf_op jit(solution)/shard_map/ppermute | solution.py:62
  60.4 7.7 %collective-permute-start.16 = (f32[4,2,64,128]{3,2,1,0:T(8,128)S(1)}, f32[4,2,64,128]{3,2,1,0:T(8,128)S(1)}, u32[]{:S(2)}, u32[]{:S(2)}) collective-permute-start(f32[4,2,64,128]{3,2,1,0:T(8,128)S(1)} %get-tuple-element.84), channel_id=1, source_target_pairs={{8,16},{16,8},{9,17},{17,9},{10,18},{18,10},{11,19},{19,11},{12,20... | collective-permute-start | bytes 786440 | tf_op jit(solution)/shard_map/ppermute | solution.py:62
  63.0 5.1 %collective-permute-start.17 = (f32[4,2,64,128]{3,2,1,0:T(8,128)S(1)}, f32[4,2,64,128]{3,2,1,0:T(8,128)S(1)}, u32[]{:S(2)}, u32[]{:S(2)}) collective-permute-start(f32[4,2,64,128]{3,2,1,0:T(8,128)S(1)} %get-tuple-element.85), channel_id=1, source_target_pairs={{0,8},{16,24},{8,0},{24,16},{1,9},{17,25},{9,1},{25,17},{2,10},{18... | collective-permute-start | bytes 786440 | tf_op jit(solution)/shard_map/ppermute | solution.py:62
  77.9 9.4 %collective-permute-start.20 = (f32[4,3,64,128]{3,2,1,0:T(8,128)S(1)}, f32[4,3,64,128]{3,2,1,0:T(8,128)S(1)}, u32[]{:S(2)}, u32[]{:S(2)}) collective-permute-start(f32[4,3,64,128]{3,2,1,0:T(8,128)S(1)} %get-tuple-element.90), channel_id=1, source_target_pairs={{8,16},{16,8},{9,17},{17,9},{10,18},{18,10},{11,19},{19,11},{12,20... | collective-permute-start | bytes 1179656 | tf_op jit(solution)/shard_map/ppermute | solution.py:62
  80.5 6.8 %collective-permute-start.21 = (f32[4,3,64,128]{3,2,1,0:T(8,128)S(1)}, f32[4,3,64,128]{3,2,1,0:T(8,128)S(1)}, u32[]{:S(2)}, u32[]{:S(2)}) collective-permute-start(f32[4,3,64,128]{3,2,1,0:T(8,128)S(1)} %get-tuple-element.91), channel_id=1, source_target_pairs={{0,8},{16,24},{8,0},{24,16},{1,9},{17,25},{9,1},{25,17},{2,10},{18... | collective-permute-start | bytes 1179656 | tf_op jit(solution)/shard_map/ppermute | solution.py:62
  80.6 9.9 %collective-permute-start.24 = (f32[4,64,128]{2,1,0:T(8,128)S(1)}, f32[4,64,128]{2,1,0:T(8,128)S(1)}, u32[]{:S(2)}, u32[]{:S(2)}) collective-permute-start(f32[4,64,128]{2,1,0:T(8,128)S(1)} %get-tuple-element.97), channel_id=1, source_target_pairs={{1,2},{3,4},{5,6},{2,1},{4,3},{6,5},{9,10},{11,12},{13,14},{10,9},... | collective-permute-start | bytes 393224 | tf_op jit(solution)/shard_map/ppermute | solution.py:62
  83.4 9.6 %collective-permute-start.25 = (f32[4,64,128]{2,1,0:T(8,128)S(1)}, f32[4,64,128]{2,1,0:T(8,128)S(1)}, u32[]{:S(2)}, u32[]{:S(2)}) collective-permute-start(f32[4,64,128]{2,1,0:T(8,128)S(1)} %get-tuple-element.98), channel_id=1, source_target_pairs={{0,1},{2,3},{4,5},{6,7},{1,0},{3,2},{5,4},{7,6},{8,9},{10,11},{12,... | collective-permute-start | bytes 393224 | tf_op jit(solution)/shard_map/ppermute | solution.py:62
  87.4 6.9 %collective-permute-start.22 = (f32[4,64,128]{2,1,0:T(8,128)S(1)}, f32[4,64,128]{2,1,0:T(8,128)S(1)}, u32[]{:S(2)}, u32[]{:S(2)}) collective-permute-start(f32[4,64,128]{2,1,0:T(8,128)S(1)} %get-tuple-element.92), channel_id=1, source_target_pairs={{1,2},{3,4},{5,6},{2,1},{4,3},{6,5},{9,10},{11,12},{13,14},{10,9},... | collective-permute-start | bytes 393224 | tf_op jit(solution)/shard_map/ppermute | solution.py:62
  90.4 6.8 %collective-permute-start.23 = (f32[4,64,128]{2,1,0:T(8,128)S(1)}, f32[4,64,128]{2,1,0:T(8,128)S(1)}, u32[]{:S(2)}, u32[]{:S(2)}) collective-permute-start(f32[4,64,128]{2,1,0:T(8,128)S(1)} %get-tuple-element.93), channel_id=1, source_target_pairs={{0,1},{2,3},{4,5},{6,7},{1,0},{3,2},{5,4},{7,6},{8,9},{10,11},{12,... | collective-permute-start | bytes 393224 | tf_op jit(solution)/shard_map/ppermute | solution.py:62
  (3 other events, 26.7 us)

commit v2 on v1

--- a/solution.py
+++ b/solution.py
@@ -103,21 +103,25 @@
 
 
 def pack_kernel(*refs):
-    count = (len(refs) - 8) // 3
-    sources, outs, targets = refs[: count + 1], refs[count + 1 : count + 8], refs[count + 8 : -count - 2]
+    count = (len(refs) - 11) // 2
+    sources, outs, targets = refs[: count + 1], refs[count + 1 : count + 8], refs[count + 8 : -3]
     turned_ref, odd_edge, even_edge, odd_mid, even_mid, row_odd, row_even = outs
-    object_ref, sems = refs[-count - 2], refs[-count - 1 :]
+    object_ref, plane_sems, sems = refs[-3:]
+    planes, rows, cols = object_ref.shape
+    plane_copies = [
+        pltpu.make_async_copy(sources[0].at[plane], object_ref.at[plane], plane_sems.at[plane])
+        for plane in range(planes)
+    ]
     copies = [
-        pltpu.make_async_copy(source, target, sem)
-        for source, target, sem in zip(sources, (object_ref, *targets), sems)
+        pltpu.make_async_copy(source, target, sems.at[at])
+        for at, (source, target) in enumerate(zip(sources[1:], targets))
     ]
-    for copy in copies:
+    for copy in plane_copies + copies:
         copy.start()
-    copies[0].wait()
-    planes, rows, cols = object_ref.shape
     tiles = cols // LANES
     pieces = segments(rows, odd_edge.shape[1])
     for plane in range(planes):
+        plane_copies[plane].wait()
         for (upper, lower), odd_ref, even_ref in zip(
             pieces, (odd_edge, odd_mid), (even_edge, even_mid)
         ):
@@ -129,13 +133,12 @@
                 object_ref[plane, lower, cols - LANES : cols],
             )
             odd_ref[plane], even_ref[plane] = paired("col", left, right)
-    for plane in range(planes):
         for tile in range(tiles):
             turned = swap_halves(object_ref[plane, :, tile * LANES : (tile + 1) * LANES])
             turned_ref[plane, tile] = turned
             upper, lower = pieces[0]
             row_odd[plane, tile], row_even[plane, tile] = paired("row", turned[upper], turned[lower])
-    for copy in copies[1:]:
+    for copy in copies:
         copy.wait()
 
 
@@ -559,8 +562,11 @@
         + [packed_edge] * 2 + [packed_mid] * 2 + [row_strip] * 2
         + [pltpu.VMEM(array.shape, array.dtype) for array in constants],
         8,
-        scratch=[f32(planes, tile_r, tile_c)]
-        + [pltpu.SemaphoreType.DMA(())] * (len(constants) + 1),
+        scratch=[
+            f32(planes, tile_r, tile_c),
+            pltpu.SemaphoreType.DMA((planes,)),
+            pltpu.SemaphoreType.DMA((len(constants),)),
+        ],
         raw=[tile, *constants],
     )()
     edge_strips = exchange(odd_edge, even_edge, "col")

time: 98.9 us -> 99 us (level)
  no operation moved by 1% of the time
where the time goes in v2:
time: 99 us; the launch traced here: 98.5 us
  starting transfers between devices  45.3 us (46%)
  waiting for transfers between devices  27.8 us (28%)
  Pallas kernels  24.5 us (25%)
  between operations  0.99 us (1%)
    ppermute x26, starting transfers between devices, exchange(): received.append(lax.ppermute(values, axis, pairs))  45.3 us
    ppermute x26, waiting for transfers between devices, exchange(): received.append(lax.ppermute(values, axis, pairs))  27.8 us
    pallas_call x10, Pallas kernels, run(): pl.pallas_call(kernel, out_shape=outs, input_output_aliases=alias or {},...  24.5 us
  transfers between devices with their start and end apart: 26, of which 10 were waited for; matrix products, arithmetic and copies ran while one was open for 0% of the time, Pallas kernels for 2%

profile of v2, /device:TPU:25, one launch (start us, length us, event | category | flops | bytes accessed | tf_op | source)
XLA Modules:
  0.0 98.5 jit_solution(6093783027028425650)
XLA Ops:
  0.0 2.1 %shard_map.73 = (f32[4,2,256,128]{3,2,1,0:T(8,128)S(1)}, f32[4,64,128]{2,1,0:T(8,128)S(1)}, f32[4,64,128]{2,1,0:T(8,128)S(1)}, f32[4,64,128]{2,1,0:T(8,128)S(1)}...) custom-call(f32[4,256,256]{2,1,0:T(8,128)} %bitcast.3, ...), custom_call_target="tpu_custom_call" | custom-call | tf_op jit(solution)/shard_map/pallas_call | solution.py:538
  2.1 3.0 %collective-permute-start = (f32[4,64,128]{2,1,0:T(8,128)S(1)}, f32[4,64,128]{2,1,0:T(8,128)S(1)}, u32[]{:S(2)}, u32[]{:S(2)}) collective-permute-start(f32[4,64,128]{2,1,0:T(8,128)S(1)} %get-tuple-element.53), channel_id=1, source_target_pairs={{1,2},{3,4},{5,6},{2,1},{4,3},{6,5},{9,10},{11,12},{13,14},{10,9},... | collective-permute-start | bytes 393224 | tf_op jit(solution)/shard_map/ppermute | solution.py:62
  5.2 3.2 %collective-permute-start.2 = (f32[4,64,128]{2,1,0:T(8,128)S(1)}, f32[4,64,128]{2,1,0:T(8,128)S(1)}, u32[]{:S(2)}, u32[]{:S(2)}) collective-permute-start(f32[4,64,128]{2,1,0:T(8,128)S(1)} %get-tuple-element.55), channel_id=1, source_target_pairs={{1,2},{3,4},{5,6},{2,1},{4,3},{6,5},{9,10},{11,12},{13,14},{10,9},... | collective-permute-start | bytes 393224 | tf_op jit(solution)/shard_map/ppermute | solution.py:62
  8.5 4.5 %collective-permute-start.4 = (f32[4,2,64,128]{3,2,1,0:T(8,128)S(1)}, f32[4,2,64,128]{3,2,1,0:T(8,128)S(1)}, u32[]{:S(2)}, u32[]{:S(2)}) collective-permute-start(f32[4,2,64,128]{3,2,1,0:T(8,128)S(1)} %get-tuple-element.57), channel_id=1, source_target_pairs={{8,16},{16,8},{9,17},{17,9},{10,18},{18,10},{11,19},{19,11},{12,20... | collective-permute-start | bytes 786440 | tf_op jit(solution)/shard_map/ppermute | solution.py:62
  13.2 2.8 %collective-permute-done.1.from_even.edge_even = f32[4,64,128]{2,1,0:T(8,128)S(1)} collective-permute-done((f32[4,64,128]{2,1,0:T(8,128)S(1)}, f32[4,64,128]{2,1,0:T(8,128)S(1)}, u32[]{:S(2)}, u32[]{:S(2)}) %collective-permute-start.1) | collective-permute-done | bytes 131104 | tf_op jit(solution)/shard_map/ppermute | solution.py:62
  16.1 3.6 %collective-permute-start.6 = (f32[4,64,128]{2,1,0:T(8,128)S(1)}, f32[4,64,128]{2,1,0:T(8,128)S(1)}, u32[]{:S(2)}, u32[]{:S(2)}) collective-permute-start(f32[4,64,128]{2,1,0:T(8,128)S(1)} %get-tuple-element.59), channel_id=1, source_target_pairs={{8,16},{16,8},{9,17},{17,9},{10,18},{18,10},{11,19},{19,11},{12,20... | collective-permute-start | bytes 393224 | tf_op jit(solution)/shard_map/ppermute | solution.py:62
  20.4 1.9 %collective-permute-done.6.corner_odd = f32[4,64,128]{2,1,0:T(8,128)S(1)} collective-permute-done((f32[4,64,128]{2,1,0:T(8,128)S(1)}, f32[4,64,128]{2,1,0:T(8,128)S(1)}, u32[]{:S(2)}, u32[]{:S(2)}) %collective-permute-start.6) | collective-permute-done | bytes 131104 | tf_op jit(solution)/shard_map/ppermute | solution.py:62
  22.4 9.6 %shard_map.75 = (f32[4,3,384,128]{3,2,1,0:T(8,128)S(1)}, f32[4,2,64,128]{3,2,1,0:T(8,128)S(1)}, f32[4,2,64,128]{3,2,1,0:T(8,128)S(1)}, f32[4,1,64,128]{3,2,1,0:T...) custom-call(s32[2,1,1,16]{3,2,1,0:T(1,128)S(1)} %copy-done, ...), custom_call_target="tpu_custom_call" | custom-call | tf_op jit(solution)/shard_map/pallas_call | solution.py:538
  32.0 3.6 %collective-permute-start.8 = (f32[4,2,64,128]{3,2,1,0:T(8,128)S(1)}, f32[4,2,64,128]{3,2,1,0:T(8,128)S(1)}, u32[]{:S(2)}, u32[]{:S(2)}) collective-permute-start(f32[4,2,64,128]{3,2,1,0:T(8,128)S(1)} %get-tuple-element.67), channel_id=1, source_target_pairs={{8,16},{16,8},{9,17},{17,9},{10,18},{18,10},{11,19},{19,11},{12,20... | collective-permute-start | bytes 786440 | tf_op jit(solution)/shard_map/ppermute | solution.py:62
  35.7 4.0 %collective-permute-done.8.row_odd = f32[4,2,64,128]{3,2,1,0:T(8,128)S(1)} collective-permute-done((f32[4,2,64,128]{3,2,1,0:T(8,128)S(1)}, f32[4,2,64,128]{3,2,1,0:T(8,128)S(1)}, u32[]{:S(2)}, u32[]{:S(2)}) %collective-permute-start.8) | collective-permute-done | bytes 262176 | tf_op jit(solution)/shard_map/ppermute | solution.py:62
  39.8 3.0 %collective-permute-start.10 = (f32[4,128,128]{2,1,0:T(8,128)S(1)}, f32[4,128,128]{2,1,0:T(8,128)S(1)}, u32[]{:S(2)}, u32[]{:S(2)}) collective-permute-start(f32[4,128,128]{2,1,0:T(8,128)S(1)} %get-tuple-element.70), channel_id=1, source_target_pairs={{1,2},{3,4},{5,6},{2,1},{4,3},{6,5},{9,10},{11,12},{13,14},{10,9},... | collective-permute-start | bytes 786440 | tf_op jit(solution)/shard_map/ppermute | solution.py:62
  42.9 3.9 %collective-permute-start.12 = (f32[4,1,64,128]{3,2,1,0:T(8,128)S(1)}, f32[4,1,64,128]{3,2,1,0:T(8,128)S(1)}, u32[]{:S(2)}, u32[]{:S(2)}) collective-permute-start(f32[4,1,64,128]{3,2,1,0:T(8,128)S(1)} %get-tuple-element.75), channel_id=1, source_target_pairs={{8,16},{16,8},{9,17},{17,9},{10,18},{18,10},{11,19},{19,11},{12,20... | collective-permute-start | bytes 393224 | tf_op jit(solution)/shard_map/ppermute | solution.py:62
  46.8 3.2 %collective-permute-start.14 = (f32[4,128,128]{2,1,0:T(8,128)S(1)}, f32[4,128,128]{2,1,0:T(8,128)S(1)}, u32[]{:S(2)}, u32[]{:S(2)}) collective-permute-start(f32[4,128,128]{2,1,0:T(8,128)S(1)} %get-tuple-element.82), channel_id=1, source_target_pairs={{1,2},{3,4},{5,6},{2,1},{4,3},{6,5},{9,10},{11,12},{13,14},{10,9},... | collective-permute-start | bytes 786440 | tf_op jit(solution)/shard_map/ppermute | solution.py:62
  51.2 3.9 %collective-permute-start.18 = (f32[4,1,64,128]{3,2,1,0:T(8,128)S(1)}, f32[4,1,64,128]{3,2,1,0:T(8,128)S(1)}, u32[]{:S(2)}, u32[]{:S(2)}) collective-permute-start(f32[4,1,64,128]{3,2,1,0:T(8,128)S(1)} %get-tuple-element.86), channel_id=1, source_target_pairs={{8,16},{16,8},{9,17},{17,9},{10,18},{18,10},{11,19},{19,11},{12,20... | collective-permute-start | bytes 393224 | tf_op jit(solution)/shard_map/ppermute | solution.py:62
  55.1 5.2 %collective-permute-done.11.from_even = f32[4,128,128]{2,1,0:T(8,128)S(1)} collective-permute-done((f32[4,128,128]{2,1,0:T(8,128)S(1)}, f32[4,128,128]{2,1,0:T(8,128)S(1)}, u32[]{:S(2)}, u32[]{:S(2)}) %collective-permute-start.11) | collective-permute-done | bytes 262176 | tf_op jit(solution)/shard_map/ppermute | solution.py:62
  60.5 2.5 %collective-permute-start.16 = (f32[4,2,64,128]{3,2,1,0:T(8,128)S(1)}, f32[4,2,64,128]{3,2,1,0:T(8,128)S(1)}, u32[]{:S(2)}, u32[]{:S(2)}) collective-permute-start(f32[4,2,64,128]{3,2,1,0:T(8,128)S(1)} %get-tuple-element.84), channel_id=1, source_target_pairs={{8,16},{16,8},{9,17},{17,9},{10,18},{18,10},{11,19},{19,11},{12,20... | collective-permute-start | bytes 786440 | tf_op jit(solution)/shard_map/ppermute | solution.py:62
  65.8 2.4 %collective-permute-done.16.row_odd = f32[4,2,64,128]{3,2,1,0:T(8,128)S(1)} collective-permute-done((f32[4,2,64,128]{3,2,1,0:T(8,128)S(1)}, f32[4,2,64,128]{3,2,1,0:T(8,128)S(1)}, u32[]{:S(2)}, u32[]{:S(2)}) %collective-permute-start.16) | collective-permute-done | bytes 262176 | tf_op jit(solution)/shard_map/ppermute | solution.py:62
  68.1 9.8 %shard_map.79 = (f32[4,3,384,128]{3,2,1,0:T(8,128)S(1)}, f32[4,3,64,128]{3,2,1,0:T(8,128)S(1)}, f32[4,3,64,128]{3,2,1,0:T(8,128)S(1)}, f32[4,3,128,128]{3,2,1,0:...) custom-call(s32[2,1,1,16]{3,2,1,0:T(1,128)S(1)} %copy-done, ...), custom_call_target="tpu_custom_call" | custom-call | tf_op jit(solution)/shard_map/pallas_call | solution.py:538
  78.0 2.6 %collective-permute-start.20 = (f32[4,3,64,128]{3,2,1,0:T(8,128)S(1)}, f32[4,3,64,128]{3,2,1,0:T(8,128)S(1)}, u32[]{:S(2)}, u32[]{:S(2)}) collective-permute-start(f32[4,3,64,128]{3,2,1,0:T(8,128)S(1)} %get-tuple-element.90), channel_id=1, source_target_pairs={{8,16},{16,8},{9,17},{17,9},{10,18},{18,10},{11,19},{19,11},{12,20... | collective-permute-start | bytes 1179656 | tf_op jit(solution)/shard_map/ppermute | solution.py:62
  80.6 2.8 %collective-permute-start.24 = (f32[4,64,128]{2,1,0:T(8,128)S(1)}, f32[4,64,128]{2,1,0:T(8,128)S(1)}, u32[]{:S(2)}, u32[]{:S(2)}) collective-permute-start(f32[4,64,128]{2,1,0:T(8,128)S(1)} %get-tuple-element.97), channel_id=1, source_target_pairs={{1,2},{3,4},{5,6},{2,1},{4,3},{6,5},{9,10},{11,12},{13,14},{10,9},... | collective-permute-start | bytes 393224 | tf_op jit(solution)/shard_map/ppermute | solution.py:62
  83.5 3.8 %collective-permute-done.20.row_odd = f32[4,3,64,128]{3,2,1,0:T(8,128)S(1)} collective-permute-done((f32[4,3,64,128]{3,2,1,0:T(8,128)S(1)}, f32[4,3,64,128]{3,2,1,0:T(8,128)S(1)}, u32[]{:S(2)}, u32[]{:S(2)}) %collective-permute-start.20) | collective-permute-done | bytes 393248 | tf_op jit(solution)/shard_map/ppermute | solution.py:62
  87.5 3.0 %collective-permute-start.22 = (f32[4,64,128]{2,1,0:T(8,128)S(1)}, f32[4,64,128]{2,1,0:T(8,128)S(1)}, u32[]{:S(2)}, u32[]{:S(2)}) collective-permute-start(f32[4,64,128]{2,1,0:T(8,128)S(1)} %get-tuple-element.92), channel_id=1, source_target_pairs={{1,2},{3,4},{5,6},{2,1},{4,3},{6,5},{9,10},{11,12},{13,14},{10,9},... | collective-permute-start | bytes 393224 | tf_op jit(solution)/shard_map/ppermute | solution.py:62
  90.6 2.5 %collective-permute-done.25.from_even = f32[4,64,128]{2,1,0:T(8,128)S(1)} collective-permute-done((f32[4,64,128]{2,1,0:T(8,128)S(1)}, f32[4,64,128]{2,1,0:T(8,128)S(1)}, u32[]{:S(2)}, u32[]{:S(2)}) %collective-permute-start.25) | collective-permute-done | bytes 131104 | tf_op jit(solution)/shard_map/ppermute | solution.py:62
  94.4 2.9 %collective-permute-done.23.from_even = f32[4,64,128]{2,1,0:T(8,128)S(1)} collective-permute-done((f32[4,64,128]{2,1,0:T(8,128)S(1)}, f32[4,64,128]{2,1,0:T(8,128)S(1)}, u32[]{:S(2)}, u32[]{:S(2)}) %collective-permute-start.23) | collective-permute-done | bytes 131104 | tf_op jit(solution)/shard_map/ppermute | solution.py:62
  (40 shorter events, 7.6 us)
Async XLA Ops:
  2.1 11.0 %collective-permute-start = (f32[4,64,128]{2,1,0:T(8,128)S(1)}, f32[4,64,128]{2,1,0:T(8,128)S(1)}, u32[]{:S(2)}, u32[]{:S(2)}) collective-permute-start(f32[4,64,128]{2,1,0:T(8,128)S(1)} %get-tuple-element.53), channel_id=1, source_target_pairs={{1,2},{3,4},{5,6},{2,1},{4,3},{6,5},{9,10},{11,12},{13,14},{10,9},... | collective-permute-start | bytes 393224 | tf_op jit(solution)/shard_map/ppermute | solution.py:62
  5.2 10.8 %collective-permute-start.1 = (f32[4,64,128]{2,1,0:T(8,128)S(1)}, f32[4,64,128]{2,1,0:T(8,128)S(1)}, u32[]{:S(2)}, u32[]{:S(2)}) collective-permute-start(f32[4,64,128]{2,1,0:T(8,128)S(1)} %get-tuple-element.54), channel_id=1, source_target_pairs={{0,1},{2,3},{4,5},{6,7},{1,0},{3,2},{5,4},{7,6},{8,9},{10,11},{12,... | collective-permute-start | bytes 393224 | tf_op jit(solution)/shard_map/ppermute | solution.py:62
  5.2 14.4 %collective-permute-start.2 = (f32[4,64,128]{2,1,0:T(8,128)S(1)}, f32[4,64,128]{2,1,0:T(8,128)S(1)}, u32[]{:S(2)}, u32[]{:S(2)}) collective-permute-start(f32[4,64,128]{2,1,0:T(8,128)S(1)} %get-tuple-element.55), channel_id=1, source_target_pairs={{1,2},{3,4},{5,6},{2,1},{4,3},{6,5},{9,10},{11,12},{13,14},{10,9},... | collective-permute-start | bytes 393224 | tf_op jit(solution)/shard_map/ppermute | solution.py:62
  8.5 13.9 %collective-permute-start.4 = (f32[4,2,64,128]{3,2,1,0:T(8,128)S(1)}, f32[4,2,64,128]{3,2,1,0:T(8,128)S(1)}, u32[]{:S(2)}, u32[]{:S(2)}) collective-permute-start(f32[4,2,64,128]{3,2,1,0:T(8,128)S(1)} %get-tuple-element.57), channel_id=1, source_target_pairs={{8,16},{16,8},{9,17},{17,9},{10,18},{18,10},{11,19},{19,11},{12,20... | collective-permute-start | bytes 786440 | tf_op jit(solution)/shard_map/ppermute | solution.py:62
  13.0 9.3 %collective-permute-start.5 = (f32[4,2,64,128]{3,2,1,0:T(8,128)S(1)}, f32[4,2,64,128]{3,2,1,0:T(8,128)S(1)}, u32[]{:S(2)}, u32[]{:S(2)}) collective-permute-start(f32[4,2,64,128]{3,2,1,0:T(8,128)S(1)} %get-tuple-element.58), channel_id=1, source_target_pairs={{0,8},{16,24},{8,0},{24,16},{1,9},{17,25},{9,1},{25,17},{2,10},{18... | collective-permute-start | bytes 786440 | tf_op jit(solution)/shard_map/ppermute | solution.py:62
  13.1 7.3 %collective-permute-start.3 = (f32[4,64,128]{2,1,0:T(8,128)S(1)}, f32[4,64,128]{2,1,0:T(8,128)S(1)}, u32[]{:S(2)}, u32[]{:S(2)}) collective-permute-start(f32[4,64,128]{2,1,0:T(8,128)S(1)} %get-tuple-element.56), channel_id=1, source_target_pairs={{0,1},{2,3},{4,5},{6,7},{1,0},{3,2},{5,4},{7,6},{8,9},{10,11},{12,... | collective-permute-start | bytes 393224 | tf_op jit(solution)/shard_map/ppermute | solution.py:62
  16.1 6.3 %collective-permute-start.6 = (f32[4,64,128]{2,1,0:T(8,128)S(1)}, f32[4,64,128]{2,1,0:T(8,128)S(1)}, u32[]{:S(2)}, u32[]{:S(2)}) collective-permute-start(f32[4,64,128]{2,1,0:T(8,128)S(1)} %get-tuple-element.59), channel_id=1, source_target_pairs={{8,16},{16,8},{9,17},{17,9},{10,18},{18,10},{11,19},{19,11},{12,20... | collective-permute-start | bytes 393224 | tf_op jit(solution)/shard_map/ppermute | solution.py:62
  32.0 7.7 %collective-permute-start.8 = (f32[4,2,64,128]{3,2,1,0:T(8,128)S(1)}, f32[4,2,64,128]{3,2,1,0:T(8,128)S(1)}, u32[]{:S(2)}, u32[]{:S(2)}) collective-permute-start(f32[4,2,64,128]{3,2,1,0:T(8,128)S(1)} %get-tuple-element.67), channel_id=1, source_target_pairs={{8,16},{16,8},{9,17},{17,9},{10,18},{18,10},{11,19},{19,11},{12,20... | collective-permute-start | bytes 786440 | tf_op jit(solution)/shard_map/ppermute | solution.py:62
  35.6 4.1 %collective-permute-start.9 = (f32[4,2,64,128]{3,2,1,0:T(8,128)S(1)}, f32[4,2,64,128]{3,2,1,0:T(8,128)S(1)}, u32[]{:S(2)}, u32[]{:S(2)}) collective-permute-start(f32[4,2,64,128]{3,2,1,0:T(8,128)S(1)} %get-tuple-element.68), channel_id=1, source_target_pairs={{0,8},{16,24},{8,0},{24,16},{1,9},{17,25},{9,1},{25,17},{2,10},{18... | collective-permute-start | bytes 786440 | tf_op jit(solution)/shard_map/ppermute | solution.py:62
  39.8 15.3 %collective-permute-start.10 = (f32[4,128,128]{2,1,0:T(8,128)S(1)}, f32[4,128,128]{2,1,0:T(8,128)S(1)}, u32[]{:S(2)}, u32[]{:S(2)}) collective-permute-start(f32[4,128,128]{2,1,0:T(8,128)S(1)} %get-tuple-element.70), channel_id=1, source_target_pairs={{1,2},{3,4},{5,6},{2,1},{4,3},{6,5},{9,10},{11,12},{13,14},{10,9},... | collective-permute-start | bytes 786440 | tf_op jit(solution)/shard_map/ppermute | solution.py:62
  42.8 17.5 %collective-permute-start.11 = (f32[4,128,128]{2,1,0:T(8,128)S(1)}, f32[4,128,128]{2,1,0:T(8,128)S(1)}, u32[]{:S(2)}, u32[]{:S(2)}) collective-permute-start(f32[4,128,128]{2,1,0:T(8,128)S(1)} %get-tuple-element.71), channel_id=1, source_target_pairs={{0,1},{2,3},{4,5},{6,7},{1,0},{3,2},{5,4},{7,6},{8,9},{10,11},{12,... | collective-permute-start | bytes 786440 | tf_op jit(solution)/shard_map/ppermute | solution.py:62
  42.9 7.1 %collective-permute-start.12 = (f32[4,1,64,128]{3,2,1,0:T(8,128)S(1)}, f32[4,1,64,128]{3,2,1,0:T(8,128)S(1)}, u32[]{:S(2)}, u32[]{:S(2)}) collective-permute-start(f32[4,1,64,128]{3,2,1,0:T(8,128)S(1)} %get-tuple-element.75), channel_id=1, source_target_pairs={{8,16},{16,8},{9,17},{17,9},{10,18},{18,10},{11,19},{19,11},{12,20... | collective-permute-start | bytes 393224 | tf_op jit(solution)/shard_map/ppermute | solution.py:62
  46.8 4.4 %collective-permute-start.13 = (f32[4,1,64,128]{3,2,1,0:T(8,128)S(1)}, f32[4,1,64,128]{3,2,1,0:T(8,128)S(1)}, u32[]{:S(2)}, u32[]{:S(2)}) collective-permute-start(f32[4,1,64,128]{3,2,1,0:T(8,128)S(1)} %get-tuple-element.76), channel_id=1, source_target_pairs={{0,8},{16,24},{8,0},{24,16},{1,9},{17,25},{9,1},{25,17},{2,10},{18... | collective-permute-start | bytes 393224 | tf_op jit(solution)/shard_map/ppermute | solution.py:62
  46.8 17.9 %collective-permute-start.14 = (f32[4,128,128]{2,1,0:T(8,128)S(1)}, f32[4,128,128]{2,1,0:T(8,128)S(1)}, u32[]{:S(2)}, u32[]{:S(2)}) collective-permute-start(f32[4,128,128]{2,1,0:T(8,128)S(1)} %get-tuple-element.82), channel_id=1, source_target_pairs={{1,2},{3,4},{5,6},{2,1},{4,3},{6,5},{9,10},{11,12},{13,14},{10,9},... | collective-permute-start | bytes 786440 | tf_op jit(solution)/shard_map/ppermute | solution.py:62
  50.0 15.7 %collective-permute-start.15 = (f32[4,128,128]{2,1,0:T(8,128)S(1)}, f32[4,128,128]{2,1,0:T(8,128)S(1)}, u32[]{:S(2)}, u32[]{:S(2)}) collective-permute-start(f32[4,128,128]{2,1,0:T(8,128)S(1)} %get-tuple-element.83), channel_id=1, source_target_pairs={{0,1},{2,3},{4,5},{6,7},{1,0},{3,2},{5,4},{7,6},{8,9},{10,11},{12,... | collective-permute-start | bytes 786440 | tf_op jit(solution)/shard_map/ppermute | solution.py:62
  51.2 11.9 %collective-permute-start.18 = (f32[4,1,64,128]{3,2,1,0:T(8,128)S(1)}, f32[4,1,64,128]{3,2,1,0:T(8,128)S(1)}, u32[]{:S(2)}, u32[]{:S(2)}) collective-permute-start(f32[4,1,64,128]{3,2,1,0:T(8,128)S(1)} %get-tuple-element.86), channel_id=1, source_target_pairs={{8,16},{16,8},{9,17},{17,9},{10,18},{18,10},{11,19},{19,11},{12,20... | collective-permute-start | bytes 393224 | tf_op jit(solution)/shard_map/ppermute | solution.py:62
  60.5 7.7 %collective-permute-start.16 = (f32[4,2,64,128]{3,2,1,0:T(8,128)S(1)}, f32[4,2,64,128]{3,2,1,0:T(8,128)S(1)}, u32[]{:S(2)}, u32[]{:S(2)}) collective-permute-start(f32[4,2,64,128]{3,2,1,0:T(8,128)S(1)} %get-tuple-element.84), channel_id=1, source_target_pairs={{8,16},{16,8},{9,17},{17,9},{10,18},{18,10},{11,19},{19,11},{12,20... | collective-permute-start | bytes 786440 | tf_op jit(solution)/shard_map/ppermute | solution.py:62
  63.0 5.1 %collective-permute-start.17 = (f32[4,2,64,128]{3,2,1,0:T(8,128)S(1)}, f32[4,2,64,128]{3,2,1,0:T(8,128)S(1)}, u32[]{:S(2)}, u32[]{:S(2)}) collective-permute-start(f32[4,2,64,128]{3,2,1,0:T(8,128)S(1)} %get-tuple-element.85), channel_id=1, source_target_pairs={{0,8},{16,24},{8,0},{24,16},{1,9},{17,25},{9,1},{25,17},{2,10},{18... | collective-permute-start | bytes 786440 | tf_op jit(solution)/shard_map/ppermute | solution.py:62
  78.0 9.4 %collective-permute-start.20 = (f32[4,3,64,128]{3,2,1,0:T(8,128)S(1)}, f32[4,3,64,128]{3,2,1,0:T(8,128)S(1)}, u32[]{:S(2)}, u32[]{:S(2)}) collective-permute-start(f32[4,3,64,128]{3,2,1,0:T(8,128)S(1)} %get-tuple-element.90), channel_id=1, source_target_pairs={{8,16},{16,8},{9,17},{17,9},{10,18},{18,10},{11,19},{19,11},{12,20... | collective-permute-start | bytes 1179656 | tf_op jit(solution)/shard_map/ppermute | solution.py:62
  80.5 6.8 %collective-permute-start.21 = (f32[4,3,64,128]{3,2,1,0:T(8,128)S(1)}, f32[4,3,64,128]{3,2,1,0:T(8,128)S(1)}, u32[]{:S(2)}, u32[]{:S(2)}) collective-permute-start(f32[4,3,64,128]{3,2,1,0:T(8,128)S(1)} %get-tuple-element.91), channel_id=1, source_target_pairs={{0,8},{16,24},{8,0},{24,16},{1,9},{17,25},{9,1},{25,17},{2,10},{18... | collective-permute-start | bytes 1179656 | tf_op jit(solution)/shard_map/ppermute | solution.py:62
  80.6 10.0 %collective-permute-start.24 = (f32[4,64,128]{2,1,0:T(8,128)S(1)}, f32[4,64,128]{2,1,0:T(8,128)S(1)}, u32[]{:S(2)}, u32[]{:S(2)}) collective-permute-start(f32[4,64,128]{2,1,0:T(8,128)S(1)} %get-tuple-element.97), channel_id=1, source_target_pairs={{1,2},{3,4},{5,6},{2,1},{4,3},{6,5},{9,10},{11,12},{13,14},{10,9},... | collective-permute-start | bytes 393224 | tf_op jit(solution)/shard_map/ppermute | solution.py:62
  83.4 9.6 %collective-permute-start.25 = (f32[4,64,128]{2,1,0:T(8,128)S(1)}, f32[4,64,128]{2,1,0:T(8,128)S(1)}, u32[]{:S(2)}, u32[]{:S(2)}) collective-permute-start(f32[4,64,128]{2,1,0:T(8,128)S(1)} %get-tuple-element.98), channel_id=1, source_target_pairs={{0,1},{2,3},{4,5},{6,7},{1,0},{3,2},{5,4},{7,6},{8,9},{10,11},{12,... | collective-permute-start | bytes 393224 | tf_op jit(solution)/shard_map/ppermute | solution.py:62
  87.5 6.9 %collective-permute-start.22 = (f32[4,64,128]{2,1,0:T(8,128)S(1)}, f32[4,64,128]{2,1,0:T(8,128)S(1)}, u32[]{:S(2)}, u32[]{:S(2)}) collective-permute-start(f32[4,64,128]{2,1,0:T(8,128)S(1)} %get-tuple-element.92), channel_id=1, source_target_pairs={{1,2},{3,4},{5,6},{2,1},{4,3},{6,5},{9,10},{11,12},{13,14},{10,9},... | collective-permute-start | bytes 393224 | tf_op jit(solution)/shard_map/ppermute | solution.py:62
  90.5 6.8 %collective-permute-start.23 = (f32[4,64,128]{2,1,0:T(8,128)S(1)}, f32[4,64,128]{2,1,0:T(8,128)S(1)}, u32[]{:S(2)}, u32[]{:S(2)}) collective-permute-start(f32[4,64,128]{2,1,0:T(8,128)S(1)} %get-tuple-element.93), channel_id=1, source_target_pairs={{0,1},{2,3},{4,5},{6,7},{1,0},{3,2},{5,4},{7,6},{8,9},{10,11},{12,... | collective-permute-start | bytes 393224 | tf_op jit(solution)/shard_map/ppermute | solution.py:62
  (3 other events, 26.7 us)
